TPU v7x, 32 devices: a whole 2x2x4 slice. The times are simulated.
32 devices in a mesh: wide: 8 (over z, x), narrow: 4 (over y, core).
Axes of the slice: x: 2, y: 2, z: 4, core: 2. Of those that a mesh axis runs over, the one named last changes fastest.
Arguments:
- tokens: bfloat16 [32768, 1024], P(('wide', 'narrow')), may hold values from -6 to 6
- seg_ids: int32 [32, 1024], P(('wide', 'narrow')), may hold values from 0 to 7, never falling along the last dimension, each value on 1 to 512 neighbouring positions
- ln_gain: bfloat16 [1024], replicated, may hold values from 0.099609375 to 1.8984375
- ln_bias: bfloat16 [1024], replicated, may hold values from -3 to 3
- w_qkv: bfloat16 [1024, 3072], replicated, may hold values from -0.1875 to 0.1875
- b_qkv: bfloat16 [3072], replicated, may hold values from -3 to 3
- w_dense: bfloat16 [1024, 1024], replicated, may hold values from -0.75 to 0.75
- w_up: bfloat16 [1024, 4096], P(None, 'narrow'), may hold values from -0.1875 to 0.1875
- b_up: bfloat16 [4096], P('narrow'), may hold values from -3 to 3
- w_down: bfloat16 [4096, 1024], P('narrow'), may hold values from -0.09375 to 0.09375
- out_bias: bfloat16 [1024], replicated, may hold values from -3 to 3
- cotangent: bfloat16 [32768, 1024], P(('wide', 'narrow')), may hold values from -6 to 6
Outputs:
- mixed: bfloat16 [32768, 1024], P(('wide', 'narrow'))
- d_tokens: bfloat16 [32768, 1024], P(('wide', 'narrow'))
- d_ln_gain: float32 [1024], P('narrow')
- d_ln_bias: float32 [1024], P('narrow')
- d_w_qkv: float32 [1024, 3072], P(None, 'narrow')
- d_b_qkv: float32 [3072], P('narrow')
- d_w_dense: float32 [1024, 1024], P('narrow')
- d_w_up: float32 [1024, 4096], P(None, 'narrow')
- d_b_up: float32 [4096], P('narrow')
- d_w_down: float32 [4096, 1024], P('narrow')
- d_out_bias: float32 [1024], P('narrow')
Inputs may be any that keep to these rules, and one draw needn't show every extreme that they name: `seg_ids`: within each sequence of 1024 tokens the document numbers never fall; each document holds 1 to 512 tokens, and one holds exactly 512.
All inputs are finite; a program needn't handle non-finite values.
Results may differ from a plain program's by a relative error of at most 0.011.
Values may be sent and summed in bfloat16 or wider, within the bound.
A program may use at most 320 MiB of HBM per device.

v0:
```python
import math

import jax
import jax.numpy as jnp
from jax import lax
from jax.sharding import PartitionSpec as P

D = 1024
HEADS = 16
HEAD = 64
ROT = 16


def positions(segments):
    index_row = jnp.arange(segments.shape[0], dtype=jnp.int32)
    change = jnp.concatenate([jnp.ones((1,), dtype=jnp.bool_), segments[1:] != segments[:-1]])
    first_index = jnp.where(change, index_row, 0)
    return index_row - lax.cummax(first_index, axis=0)


def rope_tables(position):
    half_rot = ROT // 2
    inv_freq = 1.0 / 10000.0 ** (jnp.arange(half_rot, dtype=jnp.float32) * 2.0 / ROT)
    angles = position.astype(jnp.float32)[:, None] * inv_freq[None, :]
    angles = jnp.concatenate([angles, angles], axis=1)
    return (jnp.cos(angles), jnp.sin(angles))


def rotate(tensor, cos_table, sin_table):
    half_rot = ROT // 2
    rot_part = tensor[..., :ROT]
    turned = jnp.concatenate([-rot_part[..., half_rot:], rot_part[..., :half_rot]], axis=-1)
    rot_part = rot_part * cos_table[..., None, :] + turned * sin_table[..., None, :]
    return jnp.concatenate([rot_part, tensor[..., ROT:]], axis=-1)


def unrotate(grad_in, cos_table, sin_table):
    half_rot = ROT // 2
    rot_part = grad_in[..., :ROT]
    scaled = rot_part * sin_table[..., None, :]
    turned = jnp.concatenate([scaled[..., half_rot:], -scaled[..., :half_rot]], axis=-1)
    rot_part = rot_part * cos_table[..., None, :] + turned
    return jnp.concatenate([rot_part, grad_in[..., ROT:]], axis=-1)


def masked_scores(query_block, keys_rot, seg_query, segments, query_index, key_index):
    raw_scores = jnp.einsum(
        "qhd,khd->hqk", query_block, keys_rot, preferred_element_type=jnp.float32
    ) * (1.0 / math.sqrt(HEAD))
    visible = (seg_query[:, None] == segments[None, :]) & (
        key_index[None, :] <= query_index[:, None]
    )
    return jnp.where(visible[None], raw_scores, -1e30)


def attend_forward(queries, keys_rot, values_low, segments):
    seq_len = segments.shape[0]
    block_rows = min(512, seq_len)
    key_index = jnp.arange(seq_len, dtype=jnp.int32)
    outputs = []
    norm_parts = []
    for block_start in range(0, seq_len, block_rows):
        block_end = block_start + block_rows
        scores = masked_scores(
            queries[block_start:block_end],
            keys_rot,
            segments[block_start:block_end],
            segments,
            key_index[block_start:block_end],
            key_index,
        )
        top_score = jnp.max(scores, axis=-1, keepdims=True)
        exp_scores = jnp.exp(scores - top_score)
        total = jnp.sum(exp_scores, axis=-1, keepdims=True)
        probs = exp_scores / total
        norm_parts.append((top_score + jnp.log(total))[..., 0])
        outputs.append(
            jnp.einsum(
                "hqk,khd->qhd",
                probs.astype(jnp.bfloat16),
                values_low,
                preferred_element_type=jnp.float32,
            )
        )
    return (jnp.concatenate(outputs, axis=0), jnp.concatenate(norm_parts, axis=1))


def attend_backward(
    queries, keys_rot, values_low, segments, grad_att, log_norm, cos_table, sin_table
):
    seq_len = segments.shape[0]
    block_rows = min(512, seq_len)
    score_scale = 1.0 / math.sqrt(HEAD)
    key_index = jnp.arange(seq_len, dtype=jnp.int32)
    grad_keys = jnp.zeros(keys_rot.shape, jnp.float32)
    grad_values = jnp.zeros(values_low.shape, jnp.float32)
    grad_queries = []
    for block_start in range(0, seq_len, block_rows):
        block_end = block_start + block_rows
        query_block = queries[block_start:block_end]
        grad_block = grad_att[block_start:block_end]
        scores = masked_scores(
            query_block,
            keys_rot,
            segments[block_start:block_end],
            segments,
            key_index[block_start:block_end],
            key_index,
        )
        probs = jnp.exp(scores - log_norm[:, block_start:block_end][..., None])
        grad_prob = jnp.einsum(
            "qhd,khd->hqk", grad_block, values_low, preferred_element_type=jnp.float32
        )
        row_dot = jnp.sum(grad_prob * probs, axis=-1, keepdims=True)
        grad_score = (probs * (grad_prob - row_dot)).astype(jnp.bfloat16)
        grad_queries.append(
            jnp.einsum("hqk,khd->qhd", grad_score, keys_rot, preferred_element_type=jnp.float32)
            * score_scale
        )
        grad_keys = (
            grad_keys
            + jnp.einsum(
                "hqk,qhd->khd", grad_score, query_block, preferred_element_type=jnp.float32
            )
            * score_scale
        )
        grad_values = grad_values + jnp.einsum(
            "hqk,qhd->khd",
            probs.astype(jnp.bfloat16),
            grad_block,
            preferred_element_type=jnp.float32,
        )
    grad_query = unrotate(jnp.concatenate(grad_queries, axis=0), cos_table, sin_table)
    grad_key = unrotate(grad_keys, cos_table, sin_table)
    stacked = jnp.stack([grad_query, grad_key, grad_values], axis=1)
    return stacked.reshape(seq_len, 3 * D).astype(jnp.bfloat16)


def contract_rows(left, right):
    return lax.dot_general(
        left, right, (((0,), (0,)), ((), ())), preferred_element_type=jnp.float32
    )


def contract_cols(left, right):
    return lax.dot_general(
        left, right, (((1,), (1,)), ((), ())), preferred_element_type=jnp.float32
    )


def exact_gelu(values_in):
    return jax.nn.gelu(values_in, approximate=False)


def body(
    tokens,
    seg_ids,
    ln_gain,
    ln_bias,
    w_qkv,
    b_qkv,
    w_dense,
    w_up,
    b_up,
    w_down,
    out_bias,
    cotangent,
):
    tok_rows, model_width = tokens.shape
    seq_count, seq_len = seg_ids.shape
    tok_f32 = tokens.astype(jnp.float32)
    row_mean = jnp.mean(tok_f32, axis=-1, keepdims=True)
    centered = tok_f32 - row_mean
    variance = jnp.mean(centered * centered, axis=-1, keepdims=True)
    inv_std = lax.rsqrt(variance + 1e-05)
    unit_rows = centered * inv_std
    gain_f32 = ln_gain.astype(jnp.float32)
    normed_low = (unit_rows * gain_f32 + ln_bias.astype(jnp.float32)).astype(jnp.bfloat16)
    proj = jnp.dot(normed_low, w_qkv, preferred_element_type=jnp.float32) + b_qkv.astype(
        jnp.float32
    )
    split_qkv = proj.reshape(seq_count, seq_len, 3, HEADS, HEAD)
    position = jax.vmap(positions)(seg_ids)
    cos_table, sin_table = jax.vmap(rope_tables)(position)
    queries = rotate(split_qkv[:, :, 0], cos_table, sin_table).astype(jnp.bfloat16)
    keys_rot = rotate(split_qkv[:, :, 1], cos_table, sin_table).astype(jnp.bfloat16)
    values_low = split_qkv[:, :, 2].astype(jnp.bfloat16)

    def sequence_forward(group_item):
        return attend_forward(group_item[0], group_item[1], group_item[2], group_item[3])

    attended, log_norm = lax.map(sequence_forward, (queries, keys_rot, values_low, seg_ids))
    attended_low = attended.reshape(tok_rows, model_width).astype(jnp.bfloat16)
    attn_out = jnp.dot(attended_low, w_dense, preferred_element_type=jnp.float32)
    normed_all = lax.all_gather(normed_low, "narrow", axis=0, tiled=True)
    pre_act = jnp.dot(normed_all, w_up, preferred_element_type=jnp.float32) + b_up.astype(
        jnp.float32
    )
    hidden = exact_gelu(pre_act).astype(jnp.bfloat16)
    row_piece = hidden
    partial_low = jnp.dot(row_piece, w_down, preferred_element_type=jnp.float32).astype(
        jnp.bfloat16
    )
    mlp_out = lax.psum_scatter(
        lax.optimization_barrier(partial_low).astype(jnp.float32).astype(jnp.bfloat16),
        "narrow",
        scatter_dimension=0,
        tiled=True,
    ).astype(jnp.float32)
    mixed = (tok_f32 + attn_out + mlp_out + out_bias.astype(jnp.float32)).astype(jnp.bfloat16)
    grad_f32 = cotangent.astype(jnp.float32)
    d_out_bias = jnp.sum(grad_f32, axis=0)
    d_w_dense = contract_rows(attended_low, cotangent)
    grad_att = contract_cols(cotangent, w_dense).astype(jnp.bfloat16)
    grad_att = grad_att.reshape(seq_count, seq_len, HEADS, HEAD)

    def sequence_backward(group_item):
        return attend_backward(*group_item)

    grad_proj = lax.map(
        sequence_backward,
        (queries, keys_rot, values_low, seg_ids, grad_att, log_norm, cos_table, sin_table),
    )
    grad_proj = grad_proj.reshape(tok_rows, 3 * model_width)
    d_w_qkv = contract_rows(normed_low, grad_proj)
    d_b_qkv = jnp.sum(grad_proj.astype(jnp.float32), axis=0)
    grad_normed = contract_cols(grad_proj, w_qkv)
    grad_all = lax.all_gather(cotangent, "narrow", axis=0, tiled=True)
    grad_hidden = contract_cols(grad_all, w_down)
    unused, gelu_pull = jax.vjp(exact_gelu, pre_act)
    grad_pre = gelu_pull(grad_hidden)[0].astype(jnp.bfloat16)
    d_w_down = contract_rows(hidden, grad_all)
    d_w_up = contract_rows(normed_all, grad_pre)
    d_b_up = jnp.sum(grad_pre.astype(jnp.float32), axis=0)
    row_piece = grad_pre
    partial_low = contract_cols(row_piece, w_up).astype(jnp.bfloat16)
    grad_normed = grad_normed + lax.psum_scatter(
        lax.optimization_barrier(partial_low).astype(jnp.float32).astype(jnp.bfloat16),
        "narrow",
        scatter_dimension=0,
        tiled=True,
    ).astype(jnp.float32)
    grad_unit = grad_normed * gain_f32
    d_ln_gain = jnp.sum(grad_normed * unit_rows, axis=0)
    d_ln_bias = jnp.sum(grad_normed, axis=0)
    mean_grad = jnp.mean(grad_unit, axis=-1, keepdims=True)
    mean_proj = jnp.mean(grad_unit * unit_rows, axis=-1, keepdims=True)
    d_tokens = (grad_f32 + inv_std * (grad_unit - mean_grad - unit_rows * mean_proj)).astype(
        jnp.bfloat16
    )
    shares = (
        lax.psum_scatter(
            d_w_qkv.astype(jnp.bfloat16), "narrow", scatter_dimension=1, tiled=True
        ).astype(jnp.float32),
        lax.psum_scatter(
            d_b_qkv.astype(jnp.bfloat16), "narrow", scatter_dimension=0, tiled=True
        ).astype(jnp.float32),
        lax.psum_scatter(
            d_w_dense.astype(jnp.bfloat16), "narrow", scatter_dimension=0, tiled=True
        ).astype(jnp.float32),
        lax.psum_scatter(
            d_out_bias.astype(jnp.bfloat16), "narrow", scatter_dimension=0, tiled=True
        ).astype(jnp.float32),
        lax.psum_scatter(
            d_ln_gain.astype(jnp.bfloat16), "narrow", scatter_dimension=0, tiled=True
        ).astype(jnp.float32),
        lax.psum_scatter(
            d_ln_bias.astype(jnp.bfloat16), "narrow", scatter_dimension=0, tiled=True
        ).astype(jnp.float32),
    )
    d_w_qkv, d_b_qkv, d_w_dense, d_out_bias, d_ln_gain, d_ln_bias = shares
    summed = lax.psum(
        (d_w_qkv, d_b_qkv, d_w_dense, d_out_bias, d_ln_gain, d_ln_bias, d_w_up, d_b_up, d_w_down),
        "wide",
    )
    d_w_qkv, d_b_qkv, d_w_dense, d_out_bias, d_ln_gain, d_ln_bias, d_w_up, d_b_up, d_w_down = summed
    return (
        mixed,
        d_tokens,
        d_ln_gain,
        d_ln_bias,
        d_w_qkv,
        d_b_qkv,
        d_w_dense,
        d_w_up,
        d_b_up,
        d_w_down,
        d_out_bias,
    )


def solution(mesh):
    in_specs = (
        P(("wide", "narrow"), None),
        P(("wide", "narrow"), None),
        P(),
        P(),
        P(),
        P(),
        P(),
        P(None, "narrow"),
        P("narrow"),
        P("narrow", None),
        P(),
        P(("wide", "narrow"), None),
    )
    out_specs = (
        P(("wide", "narrow"), None),
        P(("wide", "narrow"), None),
        P("narrow"),
        P("narrow"),
        P(None, "narrow"),
        P("narrow"),
        P("narrow", None),
        P(None, "narrow"),
        P("narrow"),
        P("narrow", None),
        P("narrow"),
    )
    return jax.shard_map(body, mesh=mesh, in_specs=in_specs, out_specs=out_specs, check_vma=False)
```

profile of v0, /device:TPU:0, one launch (start us, length us, event | category | flops | bytes accessed | tf_op | source)
XLA Modules:
  0.0 938.7 jit_solution(6367648714625515960)
XLA Ops:
  7.2 0.8 convert_element_type.157
  8.1 0.7 convert_element_type.158
  8.8 2.0 convert_reduce_fusion.1
  10.7 2.3 fusion.32
  13.1 0.6 copy-done.37
  13.6 3.7 fusion.25
  17.4 0.7 all-gather.5.cloned.1.call-update
  18.3 12.6 %broadcast_add_fusion = f32[1024,3072]{1,0:T(8,128)} fusion(f32[3072]{0:T(1024)S(1)} %convert_element_type.160, bf16[1024,1024]{1,0:T(8,128)(2,1)} %fusion.25, bf16[1024,3072]{1,0:T(8,128)(2,1)} %param.16), kind=kOutput, calls=%fused_computation.43 | convolution fusion | flops 6445596672 | bytes 20983808 | tf_op jit(solution)/shard_map/dot_general | solution.py:179
  30.9 13.1 %copy.27 = f32[1024,3072]{0,1:T(8,128)} copy(f32[1024,3072]{1,0:T(8,128)} %broadcast_add_fusion) | data formatting | bytes 25165824 | tf_op jit(solution)/shard_map/add | solution.py:179
  44.0 4.3 slice_bitcast_fusion
  48.4 1.5 fusion.43
  49.9 2.0 slice.245
  51.9 1.2 slice_negate_fusion.2
  54.2 1.7 fusion.39
  56.0 2.4 fusion.55
  58.4 14.0 %fusion.73 = (f32[16,512]{1,0:T(8,128)S(1)}, f32[16,512,1024]{2,1,0:T(8,128)}) fusion(bf16[1024,16,48]{0,2,1:T(8,128)(2,1)S(1)} %copy-done.3, bf16[1024,16,16]{0,2,1:T(8,128)(2,1)S(1)} %get-tuple-element.98, bf16[1,1024,16,48]{1,3,2,0:T(8,128)(2,1)S(1)} %copy-done.2, bf16[1,1024,16,16]{1,3,2,0:T(8,128)(2,1)S(1)} %get-tuple-element.99, ...), kind=kOutput, calls=%fused_computation.151 | convolution fusion | flops 1105190912 | bytes 38305792 | tf_op jit(solution)/shard_map/while/body/eval_jaxpr/qhd,khd->hqk/dot_general | solution.py:47
  72.4 14.2 %fusion.74 = (f32[16,512]{1,0:T(8,128)S(1)}, f32[16,512,1024]{2,1,0:T(8,128)}) fusion(bf16[1024,16,48]{0,2,1:T(8,128)(2,1)S(1)} %copy-done.3, bf16[1024,16,16]{0,2,1:T(8,128)(2,1)S(1)} %get-tuple-element.98, bf16[1,1024,16,16]{1,3,2,0:T(8,128)(2,1)S(1)} %get-tuple-element.99, bf16[1,1024,16,48]{1,3,2,0:T(8,128)(2,1)S(1)} %copy-done.2, ...), kind=kOutput, calls=%fused_computation.152 | convolution fusion | flops 1105190912 | bytes 38305792 | tf_op jit(solution)/shard_map/while/body/eval_jaxpr/qhd,khd->hqk/dot_general | solution.py:47
  86.6 16.8 %fusion.1 = f32[16,512]{1,0:T(8,128)S(1)} fusion(f32[16,512,1024]{2,1,0:T(8,128)} %get-tuple-element.110, f32[16,512]{1,0:T(8,128)S(1)} %get-tuple-element.109), kind=kLoop, calls=%fused_computation.13 | loop fusion | flops 16769024 | bytes 33619968 | tf_op jit(solution)/shard_map/while/body/eval_jaxpr/reduce_sum | solution.py:74
  103.5 5.8 copy-done.1
  109.3 8.2 fusion
  117.5 16.2 %fusion.47 = bf16[512,16,64]{0,2,1:T(8,128)(2,1)S(1)} fusion(f32[16,512,1024]{2,1,0:T(8,128)} %get-tuple-element.110, f32[16,512]{1,0:T(8,128)S(1)} %fusion.1, f32[16,512]{1,0:T(8,128)S(1)} %copy-done.24, f32[1,1024,3,16,64]{1,4,3,2,0:T(8,128)} %bitcast.98), kind=kOutput, calls=%fused_computation.97 | convolution fusion | flops 1099431936 | bytes 36765696 | tf_op jit(solution)/shard_map/while/body/eval_jaxpr/hqk,khd->qhd/dot_general | solution.py:78
  133.8 13.9 %fusion.46 = bf16[512,16,64]{0,2,1:T(8,128)(2,1)} fusion(f32[16,512,1024]{2,1,0:T(8,128)} %get-tuple-element.112, f32[16,512]{1,0:T(8,128)} %fusion, f32[16,512]{1,0:T(8,128)} %copy-done.26, f32[1,1024,3,16,64]{1,4,3,2,0:T(8,128)S(1)} %bitcast.103), kind=kOutput, calls=%fused_computation.96 | convolution fusion | flops 1099431936 | bytes 36765696 | tf_op jit(solution)/shard_map/while/body/eval_jaxpr/hqk,khd->qhd/dot_general | solution.py:78
  147.7 1.5 pad_maximum_fusion.1
  149.2 1.3 copy-done.16
  150.6 3.7 convolution_convert_fusion.3
  154.4 4.6 convolution_convert_fusion.4
  159.2 16.8 %fusion.5 = f32[16,64,1024]{2,1,0:T(8,128)} fusion(bf16[512,16,64]{0,2,1:T(8,128)(2,1)S(1)} %bitcast.106, f32[16,512,1024]{2,1,0:T(8,128)} %get-tuple-element.110, f32[16,512]{1,0:T(8,128)S(1)} %log_add_fusion), kind=kOutput, calls=%fused_computation.18 | convolution fusion | flops 1090519040 | bytes 38830080 | tf_op jit(solution)/shard_map/while/body/eval_jaxpr/hqk,qhd->khd/dot_general | solution.py:127
  176.0 23.9 %multiply_reduce_fusion = (f32[16,512]{1,0:T(8,128)S(1)}, f32[16,512,1024]{2,1,0:T(8,128)}) fusion(f32[16,512,1024]{2,1,0:T(8,128)} %get-tuple-element.110, f32[16,512]{1,0:T(8,128)S(1)} %log_add_fusion, bf16[512,16,64]{0,2,1:T(8,128)(2,1)S(1)} %bitcast.107, f32[1,1024,3,16,64]{1,4,3,2,0:T(8,128)} %bitcast.99), kind=kOutput, calls=%fused_computation.1 | convolution fusion | flops 1098899456 | bytes 70320128 | tf_op jit(solution)/shard_map/while/body/eval_jaxpr/qhd,khd->hqk/dot_general | solution.py:111
  199.9 23.8 %multiply_reduce_fusion.1 = (f32[16,512]{1,0:T(8,128)S(1)}, f32[16,512,1024]{2,1,0:T(8,128)}) fusion(f32[16,512,1024]{2,1,0:T(8,128)} %get-tuple-element.112, f32[16,512]{1,0:T(8,128)S(1)} %log_add_fusion.1, bf16[512,16,64]{0,2,1:T(8,128)(2,1)S(1)} %bitcast.104, f32[1,1024,3,16,64]{1,4,3,2,0:T(8,128)} %bitcast.100), kind=kOutput, calls=%fused_computation.4 | convolution fusion | flops 1098899456 | bytes 70320128 | tf_op jit(solution)/shard_map/while/body/eval_jaxpr/qhd,khd->hqk/dot_general | solution.py:111
  223.7 27.9 %multiply_convert_fusion.1 = bf16[16,512,1024]{2,1,0:T(8,128)(2,1)} fusion(f32[16,512,1024]{2,1,0:T(8,128)} %get-tuple-element.114, f32[16,512,1024]{2,1,0:T(8,128)} %get-tuple-element.112, f32[16,512]{1,0:T(8,128)S(1)} %get-tuple-element.113, f32[16,512]{1,0:T(8,128)S(1)} %log_add_fusion.1), kind=kLoop, calls=%fused_computation.3 | loop fusion | flops 33554432 | bytes 83951616 | tf_op jit(solution)/shard_map/while/body/eval_jaxpr/convert_element_type | solution.py:115
  251.6 12.9 %multiply_bitcast_fusion.2 = f32[512,16,64]{0,2,1:T(8,128)} fusion(bf16[16,512,1024]{2,1,0:T(8,128)(2,1)} %multiply_convert_fusion.1, bf16[1024,16,48]{0,2,1:T(8,128)(2,1)} %fusion.43, bf16[1024,16,16]{0,2,1:T(8,128)(2,1)} %copy-done.10), kind=kOutput, calls=%fused_computation.86 | convolution fusion | flops 1078460416 | bytes 20971520 | tf_op jit(solution)/shard_map/while/body/eval_jaxpr/hqk,khd->qhd/dot_general | solution.py:117
  264.5 11.1 %fusion.64 = f32[16,64,1024]{2,1,0:T(8,128)} fusion(bf16[16,512,1024]{2,1,0:T(8,128)(2,1)} %multiply_convert_fusion.1, bf16[1,1024,16,16]{1,3,2,0:T(8,128)(2,1)} %copy-done.9, bf16[1,1024,16,48]{1,3,2,0:T(8,128)(2,1)} %slice.245), kind=kOutput, calls=%fused_computation.145 | convolution fusion | flops 1075838976 | bytes 23068672 | tf_op jit(solution)/shard_map/while/body/eval_jaxpr/hqk,qhd->khd/dot_general | solution.py:122
  275.7 27.9 %multiply_convert_fusion = bf16[16,512,1024]{2,1,0:T(8,128)(2,1)} fusion(f32[16,512,1024]{2,1,0:T(8,128)} %get-tuple-element.116, f32[16,512,1024]{2,1,0:T(8,128)} %get-tuple-element.110, f32[16,512]{1,0:T(8,128)S(1)} %get-tuple-element.115, f32[16,512]{1,0:T(8,128)S(1)} %log_add_fusion), kind=kLoop, calls=%fused_computation | loop fusion | flops 33554432 | bytes 83951616 | tf_op jit(solution)/shard_map/while/body/eval_jaxpr/convert_element_type | solution.py:115
  303.6 12.9 %multiply_bitcast_fusion.1 = f32[512,16,64]{0,2,1:T(8,128)} fusion(bf16[16,512,1024]{2,1,0:T(8,128)(2,1)} %multiply_convert_fusion, bf16[1024,16,48]{0,2,1:T(8,128)(2,1)} %fusion.43, bf16[1024,16,16]{0,2,1:T(8,128)(2,1)} %copy-done.10), kind=kOutput, calls=%fused_computation.85 | convolution fusion | flops 1078460416 | bytes 20971520 | tf_op jit(solution)/shard_map/while/body/eval_jaxpr/hqk,khd->qhd/dot_general | solution.py:117
  316.5 10.5 %multiply_bitcast_fusion = f32[1024,16,64]{0,2,1:T(8,128)S(1)} fusion(f32[16,64,1024]{2,1,0:T(8,128)} %fusion.64, bf16[16,512,1024]{2,1,0:T(8,128)(2,1)} %multiply_convert_fusion, bf16[1,1024,16,48]{1,3,2,0:T(8,128)(2,1)} %slice.245, bf16[1,1024,16,16]{1,3,2,0:T(8,128)(2,1)} %copy-done.9), kind=kOutput, calls=%fused_computation.76 | convolution fusion | flops 1077936128 | bytes 27262976 | tf_op jit(solution)/shard_map/while/body/eval_jaxpr/hqk,qhd->khd/dot_general | solution.py:122
  328.1 0.5 maximum_add_fusion
  328.6 1.5 maximum_bitcast_fusion
  330.2 1.6 fusion.37
  331.8 16.2 %add_bitcast_fusion = bf16[1024,1,16,64]{0,3,2,1:T(8,128)(2,1)} fusion(f32[16,64,1024]{2,1,0:T(8,128)} %fusion.5, bf16[512,16,64]{0,2,1:T(8,128)(2,1)S(1)} %bitcast.105, f32[16,512,1024]{2,1,0:T(8,128)} %get-tuple-element.112, f32[16,512]{1,0:T(8,128)S(1)} %log_add_fusion.1), kind=kOutput, calls=%fused_computation.75 | convolution fusion | flops 1092616192 | bytes 40927232 | tf_op jit(solution)/shard_map/while/body/eval_jaxpr/hqk,qhd->khd/dot_general | solution.py:127
  348.0 4.6 fusion.68
  352.6 2.6 copy-done.14
  355.2 9.1 convolution_convert_fusion.2
  364.5 0.6 copy-done.40
  365.1 16.1 %fusion.79 = f32[4096,1024]{1,0:T(8,128)} fusion(bf16[4096,1024]{1,0:T(8,128)(2,1)} %all-gather.3.cloned.1.call-done, bf16[1024,1024]{1,0:T(8,128)(2,1)} %param.19), kind=kOutput, calls=%fused_computation.153 | convolution fusion | flops 8589934592 | bytes 27262976 | tf_op jit(solution)/shard_map/dot_general | solution.py:196
  381.2 50.9 %convert_reduce_fusion = (f32[1024]{0:T(1024)S(1)}, bf16[4096,1024]{1,0:T(8,128)(2,1)S(1)}, f32[4096,1024]{1,0:T(8,128)}) fusion(f32[4096,1024]{1,0:T(8,128)} %fusion.79, f32[1024]{0:T(1024)S(1)} %convert_element_type.166, bf16[4096,1024]{1,0:T(8,128)(2,1)} %all-gather.5.cloned.1.call-done, bf16[1024,1024]{1,0:T(8,128)(2,1)S(1)} %copy-done), kind=kOutput, calls=%fused_computation.20 | convolution fusion | flops 8904506368 | bytes 52436992 | tf_op jit(solution)/shard_map/dot_general | solution.py:146
  432.1 3.2 copy-done.44
  435.3 11.1 %convolution_convert_fusion = bf16[4096,1024]{1,0:T(8,128)(2,1)} fusion(bf16[4096,1024]{1,0:T(8,128)(2,1)S(1)} %get-tuple-element.80, bf16[1024,1024]{1,0:T(8,128)(2,1)S(1)} %copy-done.42), kind=kOutput, calls=%fused_computation.41 | convolution fusion | flops 8594128896 | bytes 18874368 | tf_op jit(solution)/shard_map/dot_general | solution.py:146
  446.5 13.0 %multiply_convert_fusion.2 = bf16[4096,1024]{1,0:T(8,128)(2,1)S(1)} fusion(f32[4096,1024]{1,0:T(8,128)} %get-tuple-element.81, f32[4096,1024]{1,0:T(8,128)} %fusion.79, f32[1024]{0:T(1024)S(1)} %convert_element_type.166), kind=kLoop, calls=%fused_computation.24 | loop fusion | flops 16777216 | bytes 41947136 | tf_op jit(solution)/shard_map/convert_element_type | solution.py:199
  459.5 4.5 copy-done.12
  464.0 10.8 %convolution_convert_fusion.1 = bf16[4096,1024]{1,0:T(8,128)(2,1)} fusion(bf16[4096,1024]{1,0:T(8,128)(2,1)S(1)} %multiply_convert_fusion.2, bf16[1024,1024]{1,0:T(8,128)(2,1)S(1)} %copy-done), kind=kOutput, calls=%fused_computation.42 | convolution fusion | flops 8594128896 | bytes 18874368 | tf_op jit(solution)/shard_map/dot_general | solution.py:201
  474.9 15.2 %fusion.80 = f32[1024,1024]{1,0:T(8,128)} fusion(bf16[4096,1024]{1,0:T(8,128)(2,1)} %all-gather.3.cloned.1.call-done, bf16[4096,1024]{1,0:T(8,128)(2,1)} %copy-done.44), kind=kOutput, calls=%fused_computation.154 | convolution fusion | flops 8589934592 | bytes 20971520 | tf_op jit(solution)/shard_map/dot_general | solution.py:140
  490.1 12.6 %fusion.81 = f32[1024,1024]{1,0:T(8,128)} fusion(bf16[4096,1024]{1,0:T(8,128)(2,1)S(1)} %copy-done.13, bf16[4096,1024]{1,0:T(8,128)(2,1)} %all-gather.5.cloned.1.call-done), kind=kOutput, calls=%fused_computation.155 | convolution fusion | flops 8589934592 | bytes 20971520 | tf_op jit(solution)/shard_map/dot_general | solution.py:140
  502.8 0.6 copy-done.43
  503.4 0.6 dynamic-slice.1
  505.3 2.0 reduce_sum.142
  507.4 13.7 %reduce-scatter.7.cloned.1.call-done = bf16[1024,1024]{1,0:T(8,128)(2,1)} async-done(((bf16[4096,1024]{1,0:T(8,128)(2,1)}), bf16[1024,1024]{1,0:T(8,128)(2,1)}) %reduce-scatter.7.cloned.1.call-update) | async-done | bytes 2097168 | tf_op jit(solution)/shard_map/reduce_scatter | solution.py:237
  521.0 14.4 %fusion.31 = (bf16[1024]{0:T(1024)(128)(2,1)S(1)}, f32[1024]{0:T(1024)S(1)}, f32[1024]{0:T(1024)S(1)}, bf16[1024]{0:T(1024)(128)(2,1)S(1)}, f32[1024,1024]{1,0:T(8,128)}) fusion(bf16[1024,1024]{1,0:T(8,128)(2,1)} %param.12, f32[1024]{0:T(1024)S(1)} %copy-done.38, f32[1024]{0:T(1024)S(1)} %copy-done.33, f32[1024]{0:T(1024)S(1)} %copy-done.36, ...), kind=kOutput, calls=%fused_computation.61 | convolution fusion | flops 6455029760 | bytes 20996096 | tf_op jit(solution)/shard_map/dot_general | solution.py:146
  535.5 10.4 %all-reduce.6 = (bf16[1024]{0:T(1024)(128)(2,1)S(1)}, bf16[1024]{0:T(1024)(128)(2,1)S(1)}, bf16[3072]{0:T(1024)(128)(2,1)S(1)}, bf16[1024]{0:T(1024)(128)(2,1)S(1)}) all-reduce(bf16[1024]{0:T(1024)(128)(2,1)S(1)} %get-tuple-element.52, ...), channel_id=4, replica_groups=mesh['wide'=8,'narrow'=4] {'narrow'}, use_global_device_ids=true, to_apply=%region_15.16.clone | all-reduce | flops 6144 | bytes 24576
  546.2 209.2 %all-reduce.11 = (f32[256]{0:T(256)}, f32[256]{0:T(256)}, f32[1024,768]{1,0:T(8,128)}, f32[768]{0:T(1024)}, f32[256,1024]{1,0:T(8,128)}, /*index=5*/f32[1024]{0:T(1024)}, f32[256]{0:T(256)}) all-reduce(f32[256]{0:T(256)S(1)} %dynamic-slice_convert_fusion.3, ...), channel_id=1, replica_groups=mesh['wide'=8,'narrow'=4] {'wide'}, use_global_device_ids=true, to_apply=%region_16.17 | all-reduce | flops 1051136 | bytes 6311936 | tf_op jit(solution)/shard_map/psum | solution.py:272
  755.3 5.3 fusion.30
  760.7 7.6 fusion.35
  768.3 156.2 %all-reduce.10.cloned.1.call-done = (f32[1024,1024]{1,0:T(8,128)}, f32[1024,1024]{1,0:T(8,128)}) async-done(((f32[1024,1024]{1,0:T(8,128)}, f32[1024,1024]{1,0:T(8,128)}), (f32[1024,1024]{1,0:T(8,128)}, f32[1024,1024]{1,0:T(8,128)})) %all-reduce.10.cloned.1.call-update) | async-done | bytes 8388624 | tf_op jit(solution)/shard_map/psum | solution.py:272
  924.5 4.9 copy.39
  929.4 2.0 copy.40
  (143 shorter events, 3.4 us)
Async XLA Ops:
  7.2 374.0 %copy-start = (bf16[1024,1024]{1,0:T(8,128)(2,1)S(1)}, bf16[1024,1024]{1,0:T(8,128)(2,1)}, u32[]{:S(2)}) copy-start(bf16[1024,1024]{1,0:T(8,128)(2,1)} %param.21) | copy-start | bytes 6291460
  7.2 357.9 %all-gather.3.cloned.1.call-start = ((), (), s32[]{:S(2)}) async-start(), calls=%async_computation.4 | async-start | bytes 10485760 | tf_op jit(solution)/shard_map/all_gather | solution.py:195
  8.1 5.0 copy-start.35
  8.8 9.5 %copy-start.31 = (s32[1,1024]{1,0:T(1,128)S(1)}, s32[1,1024]{1,0:T(1,128)}, u32[]{:S(2)}) copy-start(s32[1,1024]{1,0:T(1,128)} %param.13) | copy-start | bytes 12292
  8.8 9.6 %copy-start.39 = (bf16[3072]{0:T(1024)(128)(2,1)S(1)}, bf16[3072]{0:T(1024)(128)(2,1)}, u32[]{:S(2)}) copy-start(bf16[3072]{0:T(1024)(128)(2,1)} %param.17) | copy-start | bytes 18436
  10.7 2.3 copy-start.32
  13.1 0.6 copy-start.37
  17.4 363.8 %all-gather.5.cloned.1.call-start = ((), (), s32[]{:S(2)}) async-start(), calls=%async_computation.6 | async-start | bytes 10485760 | tf_op jit(solution)/shard_map/all_gather | solution.py:228
  18.2 489.2 %reduce-scatter.11.cloned.1.call-start = ((), (), s32[]{:S(2)}) async-start(), calls=%async_computation.9 | async-start | bytes 2621440 | tf_op jit(solution)/shard_map/reduce_scatter | solution.py:258
  48.4 3.5 copy-start.7
  48.4 4.7 copy-start.8
  53.9 4.5 copy-start.2
  53.9 4.5 copy-start.3
  54.2 4.1 copy-start.17
  54.2 4.1 copy-start.19
  58.4 14.0 %copy-start.9 = (bf16[1,1024,16,16]{1,3,2,0:T(8,128)(2,1)}, bf16[1,1024,16,16]{1,3,2,0:T(8,128)(2,1)S(1)}, u32[]{:S(2)}) copy-start(bf16[1,1024,16,16]{1,3,2,0:T(8,128)(2,1)S(1)} %get-tuple-element.99) | copy-start | bytes 1572868
  58.4 14.0 %copy-start.10 = (bf16[1024,16,16]{0,2,1:T(8,128)(2,1)}, bf16[1024,16,16]{0,2,1:T(8,128)(2,1)S(1)}, u32[]{:S(2)}) copy-start(bf16[1024,16,16]{0,2,1:T(8,128)(2,1)S(1)} %get-tuple-element.98) | copy-start | bytes 1572868
  58.4 14.0 %copy-start.22 = (pred[512,1024]{1,0:T(8,128)(4,1)S(1)}, pred[512,1024]{1,0:T(8,128)(4,1)}, u32[]{:S(2)}) copy-start(pred[512,1024]{1,0:T(8,128)(4,1)} %get-tuple-element.105) | copy-start | bytes 1572868
  72.4 14.2 %copy-start.23 = (f32[16,512]{1,0:T(8,128)}, f32[16,512]{1,0:T(8,128)S(1)}, u32[]{:S(2)}) copy-start(f32[16,512]{1,0:T(8,128)S(1)} %get-tuple-element.109) | copy-start | bytes 98308
  86.6 16.9 %copy-start.26 = (f32[16,512]{1,0:T(8,128)}, f32[16,512]{1,0:T(8,128)S(1)}, u32[]{:S(2)}) copy-start(f32[16,512]{1,0:T(8,128)S(1)} %get-tuple-element.111) | copy-start | bytes 98308
  86.6 22.7 %copy-start.1 = (f32[16,512,1024]{2,1,0:T(8,128)S(1)}, f32[16,512,1024]{2,1,0:T(8,128)}, u32[]{:S(2)}) copy-start(f32[16,512,1024]{2,1,0:T(8,128)} %get-tuple-element.112) | copy-start | bytes 100663296
  103.4 14.1 %copy-start.29 = (f32[16,512]{1,0:T(8,128)}, f32[16,512]{1,0:T(8,128)S(1)}, u32[]{:S(2)}) copy-start(f32[16,512]{1,0:T(8,128)S(1)} %fusion.1) | copy-start | bytes 98308
  109.3 8.2 copy-start.24
  109.3 24.5 %slice-start = ((s8[12582912]{0:T(1024)(128)(4,1)}), s8[4194304]{0:T(1024)(128)(4,1)S(1)}, s32[]{:S(2)}) async-start(s8[12582912]{0:T(1024)(128)(4,1)} %bitcast.101), calls=%async_computation.11 | async-start | bytes 8388608
  117.5 16.3 %slice-start.1 = ((s8[12582912]{0:T(1024)(128)(4,1)}), s8[4194304]{0:T(1024)(128)(4,1)S(1)}, s32[]{:S(2)}) async-start(s8[12582912]{0:T(1024)(128)(4,1)} %bitcast.101), calls=%async_computation.12 | async-start | bytes 8388608
  117.5 16.3 %slice-start.2 = ((s8[12582912]{0:T(1024)(128)(4,1)}), s8[4194304]{0:T(1024)(128)(4,1)S(1)}, s32[]{:S(2)}) async-start(s8[12582912]{0:T(1024)(128)(4,1)} %bitcast.101), calls=%async_computation.13 | async-start | bytes 8388608
  133.8 16.7 %copy-start.4 = (bf16[1024,1024]{1,0:T(8,128)(2,1)S(1)}, bf16[1024,1024]{1,0:T(8,128)(2,1)}, u32[]{:S(2)}) copy-start(bf16[1024,1024]{1,0:T(8,128)(2,1)} %param.23) | copy-start | bytes 6291460
  149.2 1.3 copy-start.16
  150.5 3.8 copy-start.25
  150.5 3.8 copy-start.30
  154.3 353.0 %reduce-scatter.9.cloned.1.call-start = ((), (), s32[]{:S(2)}) async-start(), calls=%async_computation.8 | async-start | bytes 7864320 | tf_op jit(solution)/shard_map/reduce_scatter | solution.py:252
  176.0 23.9 %copy-start.27 = (f32[16,512]{1,0:T(8,128)S(1)}, f32[16,512]{1,0:T(8,128)}, u32[]{:S(2)}) copy-start(f32[16,512]{1,0:T(8,128)} %copy-done.26) | copy-start | bytes 98308
  176.0 23.9 %copy-start.28 = (f32[16,512]{1,0:T(8,128)S(1)}, f32[16,512]{1,0:T(8,128)}, u32[]{:S(2)}) copy-start(f32[16,512]{1,0:T(8,128)} %fusion) | copy-start | bytes 98308
  316.5 10.7 %copy-start.5 = (f32[512,16,64]{0,2,1:T(8,128)S(1)}, f32[512,16,64]{0,2,1:T(8,128)}, u32[]{:S(2)}) copy-start(f32[512,16,64]{0,2,1:T(8,128)} %multiply_bitcast_fusion.2) | copy-start | bytes 6291460
  316.5 10.7 %copy-start.6 = (f32[512,16,64]{0,2,1:T(8,128)S(1)}, f32[512,16,64]{0,2,1:T(8,128)}, u32[]{:S(2)}) copy-start(f32[512,16,64]{0,2,1:T(8,128)} %multiply_bitcast_fusion.1) | copy-start | bytes 6291460
  316.5 10.7 %copy-start.18 = (f32[1024,16]{0,1:T(8,128)S(1)}, f32[1024,16]{0,1:T(8,128)}, u32[]{:S(2)}) copy-start(f32[1024,16]{0,1:T(8,128)} %copy-done.17) | copy-start | bytes 196612
  327.3 0.8 copy-start.20
  348.0 7.2 copy-start.11
  352.6 2.6 copy-start.14
  364.4 0.7 copy-start.40
  364.4 156.6 %reduce-scatter.7.cloned.1.call-start = ((), (), s32[]{:S(2)}) async-start(), calls=%async_computation.7 | async-start | bytes 10485760 | tf_op jit(solution)/shard_map/reduce_scatter | solution.py:237
  381.2 54.1 %copy-start.42 = (bf16[1024,1024]{1,0:T(8,128)(2,1)S(1)}, bf16[1024,1024]{1,0:T(8,128)(2,1)}, u32[]{:S(2)}) copy-start(bf16[1024,1024]{1,0:T(8,128)(2,1)} %param.19) | copy-start | bytes 6291460
  432.1 3.2 copy-start.44
  446.4 314.3 %reduce-scatter.5.cloned.1.call-start = ((), (), s32[]{:S(2)}) async-start(), calls=%async_computation.5 | async-start | bytes 10485760 | tf_op jit(solution)/shard_map/reduce_scatter | solution.py:204
  459.5 4.5 copy-start.12
  474.9 449.6 %all-reduce.10.cloned.1.call-start = ((), (), s32[]{:S(2)}) async-start(), calls=%async_computation.10 | async-start | bytes 16777216 | tf_op jit(solution)/shard_map/psum | solution.py:272
  474.9 15.2 %copy-start.13 = (bf16[4096,1024]{1,0:T(8,128)(2,1)S(1)}, bf16[4096,1024]{1,0:T(8,128)(2,1)}, u32[]{:S(2)}) copy-start(bf16[4096,1024]{1,0:T(8,128)(2,1)} %copy-done.12) | copy-start | bytes 25165828
  502.7 0.7 copy-start.43
  502.7 4.5 copy-start.41
  502.7 4.5 copy-start.34
  502.7 18.3 %copy-start.33 = (f32[1024]{0:T(1024)S(1)}, f32[1024]{0:T(1024)}, u32[]{:S(2)}) copy-start(f32[1024]{0:T(1024)} %copy-done.32) | copy-start | bytes 12292
  502.7 18.3 %copy-start.36 = (f32[1024]{0:T(1024)S(1)}, f32[1024]{0:T(1024)}, u32[]{:S(2)}) copy-start(f32[1024]{0:T(1024)} %copy-done.35) | copy-start | bytes 12292
  502.8 18.3 %copy-start.38 = (f32[1024]{0:T(1024)S(1)}, f32[1024]{0:T(1024)}, u32[]{:S(2)}) copy-start(f32[1024]{0:T(1024)} %copy-done.37) | copy-start | bytes 12292
  507.3 38.8 %copy-start.21 = (bf16[256,1024]{1,0:T(8,128)(2,1)S(1)}, bf16[256,1024]{1,0:T(8,128)(2,1)}, u32[]{:S(2)}) copy-start(bf16[256,1024]{1,0:T(8,128)(2,1)} %reduce-scatter.11.cloned.1.call-done) | copy-start | bytes 1572868
  924.5 4.9 copy-start.15
Sparse Core Ops, SparseCore 0:
  17.5 61.0 all-gather.2
  80.2 58.2 all-gather.4
  154.4 34.1 reduce-scatter.10
  364.5 61.1 reduce-scatter.8
  446.5 74.4 reduce-scatter.6
  523.6 71.7 reduce-scatter.4
  600.1 324.2 all-reduce.9
where the time goes:
time: 949 us; the launch traced here: 939 us
  matrix products  355 us (37%)
  blocking collectives  220 us (23%)
  waiting for transfers between devices  171 us (18%)
  other arithmetic  128 us (13%)
  local copies, waits for them, and re-layouts  48.8 us (5%)
  between operations  16.4 us (2%)
    psum x1, blocking collectives, body(): lax.psum((d_w_qkv, d_b_qkv, d_w_dense, d_out_bias, d_ln_gain, d_ln_bias,...  209 us
    psum x1, waiting for transfers between devices, body(): lax.psum((d_w_qkv, d_b_qkv, d_w_dense, d_out_bias, d_ln_gain, d_ln_bias,...  156 us
    dot_general x4, matrix products, contract_cols(): lax.dot_general(left, right, (((1,), (1,)), ((), ())), preferred_element_...  81 us
    convert_element_type x2, other arithmetic, attend_backward(): grad_score = (probs * (grad_prob - row_dot)).astype(jnp.bfloat16)  55.8 us
    dot_general x2, matrix products, attend_backward(): jnp.einsum('qhd,khd->hqk', grad_block, values_low, preferred_element_type...  47.6 us
    dot_general x4, matrix products, contract_rows(): lax.dot_general(left, right, (((0,), (0,)), ((), ())), preferred_element_...  40.7 us
    dot_general x2, matrix products, attend_backward(): jnp.einsum('hqk,qhd->khd', probs.astype(jnp.bfloat16), grad_block, prefer...  33.1 us
    dot_general x2, matrix products, attend_forward(): jnp.einsum('hqk,khd->qhd', probs.astype(jnp.bfloat16), values_low, prefer...  30.2 us
  transfers between devices with their start and end apart: 7, of which 2 were waited for; matrix products, arithmetic and copies ran while one was open for 53% of the time, Pallas kernels for 0%

commit v1 on v0

v1 whole, which is shorter than its diff:
```python
import math

import jax
import jax.numpy as jnp
from jax import lax
from jax.experimental import pallas as pl
from jax.experimental.pallas import tpu as pltpu
from jax.sharding import PartitionSpec as P

D = 1024
HEADS = 16
HEAD = 64
ROT = 16


TILE = 256
PAIR = 2 * HEAD
MAX_DOC = 512


def doc_starts(segments):
    return jnp.sum((segments[:, :, None] > segments[:, None, :]).astype(jnp.int32), axis=2)


def rope_coefs(position):
    half_rot = ROT // 2
    lane = jnp.arange(PAIR, dtype=jnp.int32) % HEAD
    inv_freq = 1.0 / 10000.0 ** ((lane % half_rot).astype(jnp.float32) * 2.0 / ROT)
    angles = position.astype(jnp.float32)[:, None] * inv_freq[None, :]
    cos, sin = jnp.cos(angles), jnp.sin(angles)
    rotated = (lane < ROT)[None, :]
    first = (lane < half_rot)[None, :]
    return (
        jnp.where(rotated, cos, 1.0),
        jnp.where(first, -sin, 0.0),
        jnp.where(rotated & ~first, sin, 0.0),
    )


def turn(t, same, down, up):
    half_rot = ROT // 2
    return (
        t * same
        + pltpu.roll(t, PAIR - half_rot, axis=1) * down
        + pltpu.roll(t, half_rot, axis=1) * up
    )


def dot_nt(left, right):
    return lax.dot_general(
        left, right, (((1,), (1,)), ((), ())), preferred_element_type=jnp.float32
    )


def dot_nn(left, right):
    return lax.dot_general(
        left, right, (((1,), (0,)), ((), ())), preferred_element_type=jnp.float32
    )


def qkv_kernel(
    x_ref, gain_ref, bias_ref, w_ref, b_ref, same_ref, down_ref, up_ref, out_ref, normed_ref
):
    step = pl.program_id(0)
    rows, cols = out_ref.shape
    blocks = (HEADS * HEAD) // cols

    @pl.when(step == 0)
    def _():
        for r in range(0, rows, TILE):
            x = x_ref[r : r + TILE, :].astype(jnp.float32)
            mean = jnp.mean(x, axis=-1, keepdims=True)
            centered = x - mean
            variance = jnp.mean(centered * centered, axis=-1, keepdims=True)
            unit = centered * lax.rsqrt(variance + 1e-05)
            normed_ref[r : r + TILE, :] = (unit * gain_ref[...] + bias_ref[...]).astype(
                jnp.bfloat16
            )

    scale = jnp.where(step < blocks, 1.0 / math.sqrt(HEAD), 1.0)
    for r in range(0, rows, TILE):
        acc = dot_nn(normed_ref[r : r + TILE, :], w_ref[...]) + b_ref[...]

        @pl.when(step < 2 * blocks)
        def _():
            same = same_ref[r : r + TILE, :]
            down = down_ref[r : r + TILE, :]
            up = up_ref[r : r + TILE, :]
            for c in range(0, cols, PAIR):
                out_ref[r : r + TILE, c : c + PAIR] = (
                    turn(acc[:, c : c + PAIR], same, down, up) * scale
                ).astype(jnp.bfloat16)

        @pl.when(step >= 2 * blocks)
        def _():
            out_ref[r : r + TILE, :] = acc.astype(jnp.bfloat16)


def project(tokens, gain, bias, w_qkv, b_qkv, coefs):
    rows, width = tokens.shape
    cols = 512
    whole = lambda shape: pl.BlockSpec(shape, lambda j: (0, 0))
    return pl.pallas_call(
        qkv_kernel,
        grid=(w_qkv.shape[1] // cols,),
        in_specs=[
            whole((rows, width)),
            whole((1, width)),
            whole((1, width)),
            pl.BlockSpec((width, cols), lambda j: (0, j)),
            pl.BlockSpec((1, cols), lambda j: (0, j)),
            whole((rows, PAIR)),
            whole((rows, PAIR)),
            whole((rows, PAIR)),
        ],
        out_specs=[pl.BlockSpec((rows, cols), lambda j: (0, j)), whole((rows, width))],
        out_shape=[
            jax.ShapeDtypeStruct((rows, w_qkv.shape[1]), jnp.bfloat16),
            jax.ShapeDtypeStruct((rows, width), jnp.bfloat16),
        ],
        compiler_params=pltpu.CompilerParams(vmem_limit_bytes=40 << 20),
        cost_estimate=pl.CostEstimate(
            flops=2 * rows * width * w_qkv.shape[1],
            bytes_accessed=2 * (rows * width * 2 + width * w_qkv.shape[1] * 2),
            transcendentals=0,
        ),
    )(tokens, gain, bias, w_qkv, b_qkv, *coefs)


def attention_kernel(
    first_ref,
    start_ref,
    q_ref,
    k_ref,
    v_ref,
    g_ref,
    same_ref,
    down_ref,
    up_ref,
    att_ref,
    grad_ref,
    dk_acc,
    dv_acc,
    kt_ref,
    vt_ref,
):
    rows = q_ref.shape[0]
    lane = lax.broadcasted_iota(jnp.int32, (1, PAIR), 1)
    dk_acc[...] = jnp.zeros_like(dk_acc)
    dv_acc[...] = jnp.zeros_like(dv_acc)
    kt_ref[...] = k_ref[...].astype(jnp.float32).T.astype(jnp.bfloat16)
    vt_ref[...] = v_ref[...].astype(jnp.float32).T.astype(jnp.bfloat16)

    def one_block(block, first, count):
        at = pl.multiple_of(block * TILE, TILE)
        here = pl.ds(at, TILE)
        q_pair, g_pair = q_ref[here, :], g_ref[here, :]
        start = start_ref[:, here]
        query_index = at + lax.broadcasted_iota(jnp.int32, (1, TILE), 1)
        keys = [
            pl.ds(pl.multiple_of((first + j) * TILE, TILE), TILE) for j in range(count)
        ]
        key_index = [
            (first + j) * TILE + lax.broadcasted_iota(jnp.int32, (TILE, TILE), 0)
            for j in range(count)
        ]
        visible = [(idx >= start) & (idx <= query_index) for idx in key_index]
        out_t, dq_t = [], []
        for head in range(2):
            mine = (lane >= head * HEAD) & (lane < (head + 1) * HEAD)
            q = jnp.where(mine, q_pair, jnp.zeros_like(q_pair))
            g = jnp.where(mine, g_pair, jnp.zeros_like(g_pair))
            wide = slice(head * HEAD, (head + 1) * HEAD)
            scores = [
                jnp.where(visible[j], dot_nt(k_ref[keys[j], :], q), -1e30) for j in range(count)
            ]
            grad_prob = [dot_nt(v_ref[keys[j], :], g) for j in range(count)]
            top = jnp.max(scores[0], axis=0, keepdims=True)
            for j in range(1, count):
                top = jnp.maximum(top, jnp.max(scores[j], axis=0, keepdims=True))
            exps = [jnp.exp(s - top) for s in scores]
            total = sum(jnp.sum(e, axis=0, keepdims=True) for e in exps)
            inverse = 1.0 / total
            probs = [e * inverse for e in exps]
            row_dot = sum(
                jnp.sum(p * d, axis=0, keepdims=True) for p, d in zip(probs, grad_prob)
            )
            out_head = jnp.zeros((HEAD, TILE), jnp.float32)
            dq_head = jnp.zeros((HEAD, TILE), jnp.float32)
            for j in range(count):
                low = probs[j].astype(jnp.bfloat16)
                grad_score = (probs[j] * (grad_prob[j] - row_dot)).astype(jnp.bfloat16)
                out_head += dot_nn(vt_ref[wide, keys[j]], low)
                dq_head += dot_nn(kt_ref[wide, keys[j]], grad_score)
                dv_acc[keys[j], :] += dot_nn(low, g)
                dk_acc[keys[j], :] += dot_nn(grad_score, q)
            out_t.append(out_head)
            dq_t.append(dq_head)
        att_ref[here, :] = jnp.concatenate(out_t, axis=0).T.astype(jnp.bfloat16)
        dq = jnp.concatenate(dq_t, axis=0).T * (1.0 / math.sqrt(HEAD))
        grad_ref[0, here, :] = turn(
            dq, same_ref[here, :], -down_ref[here, :], -up_ref[here, :]
        ).astype(jnp.bfloat16)

    span = MAX_DOC // TILE + 1

    def step(block, carry):
        first = first_ref[block]
        count = block + 1 - first
        for n in range(1, span + 1):

            @pl.when(count == n)
            def _(n=n):
                one_block(block, first, n)

        return carry

    lax.fori_loop(0, rows // TILE, step, 0)
    grad_ref[1] = turn(dk_acc[...], same_ref[...], -down_ref[...], -up_ref[...]).astype(
        jnp.bfloat16
    )
    grad_ref[2] = dv_acc[...].astype(jnp.bfloat16)


def attend(qkv, grad_att, starts, coefs):
    rows = qkv.shape[0]
    width = HEADS * HEAD
    pairs = width // PAIR
    first = starts[::TILE] // TILE
    whole = pl.BlockSpec((rows, PAIR), lambda i, f: (0, 0))
    return pl.pallas_call(
        attention_kernel,
        grid_spec=pltpu.PrefetchScalarGridSpec(
            num_scalar_prefetch=1,
            grid=(pairs,),
            in_specs=[
                pl.BlockSpec((1, rows), lambda i, f: (0, 0)),
                pl.BlockSpec((rows, PAIR), lambda i, f: (0, i)),
                pl.BlockSpec((rows, PAIR), lambda i, f: (0, pairs + i)),
                pl.BlockSpec((rows, PAIR), lambda i, f: (0, 2 * pairs + i)),
                pl.BlockSpec((rows, PAIR), lambda i, f: (0, i)),
                whole,
                whole,
                whole,
            ],
            out_specs=[
                pl.BlockSpec((rows, PAIR), lambda i, f: (0, i)),
                pl.BlockSpec((3, rows, PAIR), lambda i, f: (0, 0, i)),
            ],
            scratch_shapes=[
                pltpu.VMEM((rows, PAIR), jnp.float32),
                pltpu.VMEM((rows, PAIR), jnp.float32),
                pltpu.VMEM((PAIR, rows), jnp.bfloat16),
                pltpu.VMEM((PAIR, rows), jnp.bfloat16),
            ],
        ),
        out_shape=[
            jax.ShapeDtypeStruct((rows, width), jnp.bfloat16),
            jax.ShapeDtypeStruct((3, rows, width), jnp.bfloat16),
        ],
        compiler_params=pltpu.CompilerParams(vmem_limit_bytes=40 << 20),
        cost_estimate=pl.CostEstimate(
            flops=16 * rows * rows * width, bytes_accessed=16 * rows * width, transcendentals=0
        ),
    )(first, starts[None, :], qkv, qkv, qkv, grad_att, *coefs)


def contract_rows(left, right):
    return lax.dot_general(
        left, right, (((0,), (0,)), ((), ())), preferred_element_type=jnp.float32
    )


def contract_cols(left, right):
    return lax.dot_general(
        left, right, (((1,), (1,)), ((), ())), preferred_element_type=jnp.float32
    )


def exact_gelu(values_in):
    return jax.nn.gelu(values_in, approximate=False)


def body(
    tokens,
    seg_ids,
    ln_gain,
    ln_bias,
    w_qkv,
    b_qkv,
    w_dense,
    w_up,
    b_up,
    w_down,
    out_bias,
    cotangent,
):
    tok_rows, model_width = tokens.shape
    seq_count, seq_len = seg_ids.shape
    tok_f32 = tokens.astype(jnp.float32)
    row_mean = jnp.mean(tok_f32, axis=-1, keepdims=True)
    centered = tok_f32 - row_mean
    variance = jnp.mean(centered * centered, axis=-1, keepdims=True)
    inv_std = lax.rsqrt(variance + 1e-05)
    unit_rows = centered * inv_std
    gain_f32 = ln_gain.astype(jnp.float32)
    starts = doc_starts(seg_ids)
    position = jnp.arange(seq_len, dtype=jnp.int32)[None, :] - starts
    grad_att = contract_cols(cotangent, w_dense).astype(jnp.bfloat16)
    pieces = []
    for s in range(seq_count):
        part = slice(s * seq_len, (s + 1) * seq_len)
        coefs = rope_coefs(position[s])
        qkv, normed_part = project(
            tokens[part],
            gain_f32[None, :],
            ln_bias.astype(jnp.float32)[None, :],
            w_qkv,
            b_qkv.astype(jnp.float32)[None, :],
            coefs,
        )
        att_part, grad_part = attend(qkv, grad_att[part], starts[s], coefs)
        pieces.append((normed_part, att_part, grad_part))
    normed_low, attended_low = (
        jnp.concatenate([p[i] for p in pieces], axis=0) for i in range(2)
    )
    grad_proj = jnp.concatenate([p[2] for p in pieces], axis=1)
    grad_proj = jnp.concatenate([grad_proj[i] for i in range(3)], axis=1)
    attn_out = jnp.dot(attended_low, w_dense, preferred_element_type=jnp.float32)
    normed_all = lax.all_gather(normed_low, "narrow", axis=0, tiled=True)
    pre_act = jnp.dot(normed_all, w_up, preferred_element_type=jnp.float32) + b_up.astype(
        jnp.float32
    )
    hidden = exact_gelu(pre_act).astype(jnp.bfloat16)
    row_piece = hidden
    partial_low = jnp.dot(row_piece, w_down, preferred_element_type=jnp.float32).astype(
        jnp.bfloat16
    )
    mlp_out = lax.psum_scatter(
        lax.optimization_barrier(partial_low).astype(jnp.float32).astype(jnp.bfloat16),
        "narrow",
        scatter_dimension=0,
        tiled=True,
    ).astype(jnp.float32)
    mixed = (tok_f32 + attn_out + mlp_out + out_bias.astype(jnp.float32)).astype(jnp.bfloat16)
    grad_f32 = cotangent.astype(jnp.float32)
    d_out_bias = jnp.sum(grad_f32, axis=0)
    d_w_dense = contract_rows(attended_low, cotangent)
    d_w_qkv = contract_rows(normed_low, grad_proj)
    d_b_qkv = jnp.sum(grad_proj.astype(jnp.float32), axis=0)
    grad_normed = contract_cols(grad_proj, w_qkv)
    grad_all = lax.all_gather(cotangent, "narrow", axis=0, tiled=True)
    grad_hidden = contract_cols(grad_all, w_down)
    unused, gelu_pull = jax.vjp(exact_gelu, pre_act)
    grad_pre = gelu_pull(grad_hidden)[0].astype(jnp.bfloat16)
    d_w_down = contract_rows(hidden, grad_all)
    d_w_up = contract_rows(normed_all, grad_pre)
    d_b_up = jnp.sum(grad_pre.astype(jnp.float32), axis=0)
    row_piece = grad_pre
    partial_low = contract_cols(row_piece, w_up).astype(jnp.bfloat16)
    grad_normed = grad_normed + lax.psum_scatter(
        lax.optimization_barrier(partial_low).astype(jnp.float32).astype(jnp.bfloat16),
        "narrow",
        scatter_dimension=0,
        tiled=True,
    ).astype(jnp.float32)
    grad_unit = grad_normed * gain_f32
    d_ln_gain = jnp.sum(grad_normed * unit_rows, axis=0)
    d_ln_bias = jnp.sum(grad_normed, axis=0)
    mean_grad = jnp.mean(grad_unit, axis=-1, keepdims=True)
    mean_proj = jnp.mean(grad_unit * unit_rows, axis=-1, keepdims=True)
    d_tokens = (grad_f32 + inv_std * (grad_unit - mean_grad - unit_rows * mean_proj)).astype(
        jnp.bfloat16
    )
    shares = (
        lax.psum_scatter(
            d_w_qkv.astype(jnp.bfloat16), "narrow", scatter_dimension=1, tiled=True
        ).astype(jnp.float32),
        lax.psum_scatter(
            d_b_qkv.astype(jnp.bfloat16), "narrow", scatter_dimension=0, tiled=True
        ).astype(jnp.float32),
        lax.psum_scatter(
            d_w_dense.astype(jnp.bfloat16), "narrow", scatter_dimension=0, tiled=True
        ).astype(jnp.float32),
        lax.psum_scatter(
            d_out_bias.astype(jnp.bfloat16), "narrow", scatter_dimension=0, tiled=True
        ).astype(jnp.float32),
        lax.psum_scatter(
            d_ln_gain.astype(jnp.bfloat16), "narrow", scatter_dimension=0, tiled=True
        ).astype(jnp.float32),
        lax.psum_scatter(
            d_ln_bias.astype(jnp.bfloat16), "narrow", scatter_dimension=0, tiled=True
        ).astype(jnp.float32),
    )
    d_w_qkv, d_b_qkv, d_w_dense, d_out_bias, d_ln_gain, d_ln_bias = shares
    summed = lax.psum(
        (d_w_qkv, d_b_qkv, d_w_dense, d_out_bias, d_ln_gain, d_ln_bias, d_w_up, d_b_up, d_w_down),
        "wide",
    )
    d_w_qkv, d_b_qkv, d_w_dense, d_out_bias, d_ln_gain, d_ln_bias, d_w_up, d_b_up, d_w_down = summed
    return (
        mixed,
        d_tokens,
        d_ln_gain,
        d_ln_bias,
        d_w_qkv,
        d_b_qkv,
        d_w_dense,
        d_w_up,
        d_b_up,
        d_w_down,
        d_out_bias,
    )


def solution(mesh):
    in_specs = (
        P(("wide", "narrow"), None),
        P(("wide", "narrow"), None),
        P(),
        P(),
        P(),
        P(),
        P(),
        P(None, "narrow"),
        P("narrow"),
        P("narrow", None),
        P(),
        P(("wide", "narrow"), None),
    )
    out_specs = (
        P(("wide", "narrow"), None),
        P(("wide", "narrow"), None),
        P("narrow"),
        P("narrow"),
        P(None, "narrow"),
        P("narrow"),
        P("narrow", None),
        P(None, "narrow"),
        P("narrow"),
        P("narrow", None),
        P("narrow"),
    )
    return jax.shard_map(body, mesh=mesh, in_specs=in_specs, out_specs=out_specs, check_vma=False)
```

time: 949 us -> 754 us (0.79)
  matrix products: 355 us -> 157 us
  other arithmetic: 128 us -> 33.1 us
  Pallas kernels: 0 us -> 81.2 us
  waiting for transfers between devices: 171 us -> 208 us
  local copies, waits for them, and re-layouts: 48.8 us -> 31.1 us
    dot_general x13 -> x0, matrix products: 199 us -> none  [the longest x2 47.6 us: attend_backward(): jnp.einsum('qhd,khd->hqk', grad_block, values_low, preferred_element_type...]
    pallas_call x0 -> x2, Pallas kernels: none -> 81.2 us  [the longest x1 61.3 us: attend(): pl.pallas_call(attention_kernel, grid_spec=pltpu.PrefetchScalarGridSpec(n...]
    convert_element_type x6 -> x1, other arithmetic: 60.2 us -> 0.01 us  [rope_coefs(): angles = position.astype(jnp.float32)[:, None] * inv_freq[None, :]]
    reduce_sum x2 -> x1, other arithmetic: 25 us -> 1.39 us  [doc_starts(): jnp.sum((segments[:, :, None] > segments[:, None, :]).astype(jnp.int32),...]
    reduce_scatter x2, waiting for transfers between devices: 13.7 us -> 36.3 us  [body(): lax.psum_scatter(lax.optimization_barrier(partial_low).astype(jnp.float32...]
    all_gather x1, waiting for transfers between devices: 0.01 us -> 13.3 us  [body(): grad_all = lax.all_gather(cotangent, 'narrow', axis=0, tiled=True)]
    add x1 -> x0, local copies, waits for them, and re-layouts: 13.1 us -> none  [body(): jnp.dot(normed_low, w_qkv, preferred_element_type=jnp.float32)]
    unnamed x99 -> x51, local copies, waits for them, and re-layouts: 27 us -> 27.3 us
  transfers between devices with their start and end apart: 7 -> 7, of which waited for: 2 -> 3; matrix products, arithmetic and copies ran while one was open for 53% -> 25% of each run, Pallas kernels for 0% -> 8%
where the time goes in v1:
time: 754 us; the launch traced here: 748 us
  blocking collectives  220 us (29%)
  waiting for transfers between devices  208 us (28%)
  matrix products  157 us (21%)
  Pallas kernels  81.2 us (11%)
  other arithmetic  33.1 us (4%)
  local copies, waits for them, and re-layouts  31.1 us (4%)
  between operations  15.9 us (2%)
    psum x1, blocking collectives, body(): lax.psum((d_w_qkv, d_b_qkv, d_w_dense, d_out_bias, d_ln_gain, d_ln_bias,...  210 us
    psum x1, waiting for transfers between devices, body(): lax.psum((d_w_qkv, d_b_qkv, d_w_dense, d_out_bias, d_ln_gain, d_ln_bias,...  158 us
    dot_general x4, matrix products, contract_cols(): lax.dot_general(left, right, (((1,), (1,)), ((), ())), preferred_element_...  80.6 us
    pallas_call x1, Pallas kernels, attend(): pl.pallas_call(attention_kernel, grid_spec=pltpu.PrefetchScalarGridSpec(n...  61.3 us
    dot_general x4, matrix products, contract_rows(): lax.dot_general(left, right, (((0,), (0,)), ((), ())), preferred_element_...  42.5 us
    reduce_scatter x2, waiting for transfers between devices, body(): lax.psum_scatter(lax.optimization_barrier(partial_low).astype(jnp.float32...  36.3 us
    unnamed x51, local copies, waits for them, and re-layouts  27.3 us
    pallas_call x1, Pallas kernels, project(): pl.pallas_call(qkv_kernel, grid=(w_qkv.shape[1] // cols,), in_specs=[whol...  20 us
  transfers between devices with their start and end apart: 7, of which 3 were waited for; matrix products, arithmetic and copies ran while one was open for 25% of the time, Pallas kernels for 8%

profile of v1, /device:TPU:0, one launch (start us, length us, event | category | flops | bytes accessed | tf_op | source)
XLA Modules:
  0.0 748.1 jit_solution(16563470178066658632)
XLA Ops:
  7.2 0.0 all-gather.3.cloned.1.call-start
  7.3 1.4 convert_reduce_fusion.2
  8.7 0.7 convert_element_type.111
  9.4 0.7 broadcast_in_dim.63
  10.1 0.7 broadcast_in_dim.64
  10.7 2.0 fusion.21
  12.7 1.8 copy-done.1
  14.5 20.0 %shard_map.206 = (bf16[1024,3072]{1,0:T(8,128)(2,1)S(1)}, bf16[1024,1024]{1,0:T(8,128)(2,1)S(1)}) custom-call(bf16[1024,1024]{1,0:T(8,128)(2,1)S(1)} %copy-done.1, f32[1,1024]{1,0:T(1,128)S(1)} %bitcast.32, f32[1,1024]{1,0:T(1,128)S(1)} %bitcast.35, bf16[1024,3072]{1,0:T(8,128)(2,1)} %w_ref.1, f32[1,3072]{1,0:T(1,128)S(1)} %bitcast.34, ...), custom_call_target="tpu_custom_call" | custom-call | flops 6442450944 | bytes 16777216 | tf_op jit(solution)/shard_map/pallas_call | solution.py:103
  34.5 1.3 copy-done.3
  35.8 2.6 copy-done.9
  38.5 0.0 all-gather.3.cloned.1.call-update
  38.5 0.0 all-gather.5.cloned.1.call-start
  38.5 0.7 all-gather.5.cloned.1.call-update
  39.2 0.6 reduce-scatter.11.cloned.1.call-start
  39.8 0.1 slice.12
  39.9 4.7 convolution_convert_fusion.4.g_ref
  44.6 61.3 %shard_map.207 = (bf16[1024,1024]{1,0:T(8,128)(2,1)S(1)}, bf16[3,1024,1024]{2,1,0:T(8,128)(2,1)S(1)}) custom-call(s32[4]{0:T(128)S(1)} %and_select_fusion.2.first_ref, s32[1,1024]{1,0:T(1,128)S(1)} %bitcast.33, bf16[1024,3072]{1,0:T(8,128)(2,1)} %copy-done.9, bf16[1024,3072]{1,0:T(8,128)(2,1)} %copy-done.9, bf16[1024,3072]{1,0:T(8,128)(2,1)} %copy-done.9, ...), custom_call_target="tpu_custom_call" | custom-call | flops 17179869184 | bytes 16777216 | tf_op jit(solution)/shard_map/pallas_call | solution.py:231
  105.9 2.9 copy-done.2
  108.8 1.3 copy-done.10
  110.2 3.8 convolution_convert_fusion.3
  113.9 0.0 reduce-scatter.11.cloned.1.call-update
  114.0 0.2 reduce-scatter.9.cloned.1.call-start
  114.2 3.7 slice_bitcast_fusion.2
  117.9 1.3 copy-done.12
  119.2 0.7 copy-done.13
  119.9 0.7 copy-done.14
  120.6 9.3 %convolution_convert_fusion.2 = bf16[1024,3072]{1,0:T(8,128)(2,1)} fusion(bf16[1024,1024]{1,0:T(8,128)(2,1)S(1)} %copy-done.4, bf16[1024,1024]{1,0:T(8,128)(2,1)S(1)} %get-tuple-element.40, bf16[1024,1024]{1,0:T(8,128)(2,1)S(1)} %get-tuple-element.41, bf16[1024,1024]{1,0:T(8,128)(2,1)S(1)} %get-tuple-element.39), kind=kOutput, calls=%fused_computation.24 | convolution fusion | flops 6464471040 | bytes 14680064 | tf_op jit(solution)/shard_map/dot_general | solution.py:269
  129.9 0.0 reduce-scatter.9.cloned.1.call-update
  130.0 0.0 reduce-scatter.7.cloned.1.call-start
  130.0 0.0 all-gather.3.cloned.1.call-done
  130.1 16.2 %fusion.32 = f32[4096,1024]{1,0:T(8,128)} fusion(bf16[4096,1024]{1,0:T(8,128)(2,1)} %all-gather.3.cloned.1.call-done, bf16[1024,1024]{1,0:T(8,128)(2,1)} %param.19), kind=kOutput, calls=%fused_computation.80 | convolution fusion | flops 8589934592 | bytes 27262976 | tf_op jit(solution)/shard_map/dot_general | solution.py:331
  146.2 13.3 %all-gather.5.cloned.1.call-done = bf16[4096,1024]{1,0:T(8,128)(2,1)} async-done(((bf16[1024,1024]{1,0:T(8,128)(2,1)}), bf16[4096,1024]{1,0:T(8,128)(2,1)}) %all-gather.5.cloned.1.call-update) | async-done | bytes 8388624 | tf_op jit(solution)/shard_map/all_gather | solution.py:352
  159.5 50.9 %convert_reduce_fusion = (f32[1024]{0:T(1024)S(1)}, bf16[4096,1024]{1,0:T(8,128)(2,1)S(1)}, f32[4096,1024]{1,0:T(8,128)}) fusion(f32[4096,1024]{1,0:T(8,128)} %fusion.32, f32[1024]{0:T(1024)S(1)} %convert_element_type.115, bf16[4096,1024]{1,0:T(8,128)(2,1)} %all-gather.5.cloned.1.call-done, bf16[1024,1024]{1,0:T(8,128)(2,1)S(1)} %copy-done), kind=kOutput, calls=%fused_computation.2 | convolution fusion | flops 8904506368 | bytes 52436992 | tf_op jit(solution)/shard_map/dot_general | solution.py:275
  210.4 3.2 copy-done.23
  213.6 11.1 %convolution_convert_fusion = bf16[4096,1024]{1,0:T(8,128)(2,1)} fusion(bf16[4096,1024]{1,0:T(8,128)(2,1)S(1)} %get-tuple-element.37, bf16[1024,1024]{1,0:T(8,128)(2,1)S(1)} %copy-done.21), kind=kOutput, calls=%fused_computation.18 | convolution fusion | flops 8594128896 | bytes 18874368 | tf_op jit(solution)/shard_map/dot_general | solution.py:275
  224.7 0.0 reduce-scatter.7.cloned.1.call-update
  224.7 0.0 reduce-scatter.5.cloned.1.call-start
  224.8 11.8 %multiply_convert_fusion = bf16[4096,1024]{1,0:T(8,128)(2,1)S(1)} fusion(f32[4096,1024]{1,0:T(8,128)} %get-tuple-element.38, f32[4096,1024]{1,0:T(8,128)} %fusion.32, f32[1024]{0:T(1024)S(1)} %convert_element_type.115), kind=kLoop, calls=%fused_computation.4 | loop fusion | flops 16777216 | bytes 41947136 | tf_op jit(solution)/shard_map/convert_element_type | solution.py:334
  236.6 3.2 copy-done.15
  239.8 10.8 %convolution_convert_fusion.1 = bf16[4096,1024]{1,0:T(8,128)(2,1)} fusion(bf16[4096,1024]{1,0:T(8,128)(2,1)S(1)} %multiply_convert_fusion, bf16[1024,1024]{1,0:T(8,128)(2,1)S(1)} %copy-done), kind=kOutput, calls=%fused_computation.19 | convolution fusion | flops 8594128896 | bytes 18874368 | tf_op jit(solution)/shard_map/dot_general | solution.py:336
  250.6 0.0 all-reduce.10.cloned.1.call-start
  250.7 15.8 %fusion.33 = f32[1024,1024]{1,0:T(8,128)} fusion(bf16[4096,1024]{1,0:T(8,128)(2,1)} %all-gather.3.cloned.1.call-done, bf16[4096,1024]{1,0:T(8,128)(2,1)} %copy-done.23), kind=kOutput, calls=%fused_computation.81 | convolution fusion | flops 8589934592 | bytes 20971520 | tf_op jit(solution)/shard_map/dot_general | solution.py:269
  266.5 13.6 %fusion.34 = f32[1024,1024]{1,0:T(8,128)} fusion(bf16[4096,1024]{1,0:T(8,128)(2,1)S(1)} %copy-done.16, bf16[4096,1024]{1,0:T(8,128)(2,1)} %all-gather.5.cloned.1.call-done), kind=kOutput, calls=%fused_computation.82 | convolution fusion | flops 8589934592 | bytes 20971520 | tf_op jit(solution)/shard_map/dot_general | solution.py:269
  280.1 0.6 copy-done.22
  280.8 0.6 dynamic-slice
  282.6 2.0 reduce_sum.108
  284.6 1.9 convert_reduce_fusion.1
  286.6 2.3 fusion.17
  288.9 4.0 fusion.30
  292.9 0.0 reduce-scatter.11.cloned.1.call-done
  292.9 0.0 reduce-scatter.9.cloned.1.call-done
  293.0 36.3 %reduce-scatter.7.cloned.1.call-done = bf16[1024,1024]{1,0:T(8,128)(2,1)} async-done(((bf16[4096,1024]{1,0:T(8,128)(2,1)}), bf16[1024,1024]{1,0:T(8,128)(2,1)}) %reduce-scatter.7.cloned.1.call-update) | async-done | bytes 2097168 | tf_op jit(solution)/shard_map/reduce_scatter | solution.py:361
  329.2 14.0 %fusion.16 = (bf16[1024]{0:T(1024)(128)(2,1)S(1)}, f32[1024]{0:T(1024)S(1)}, f32[1024]{0:T(1024)S(1)}, bf16[1024]{0:T(1024)(128)(2,1)S(1)}, f32[1024,1024]{1,0:T(8,128)}) fusion(bf16[1024,1024]{1,0:T(8,128)(2,1)} %x_ref.1, f32[1024]{0:T(1024)S(1)} %add_rsqrt_fusion, f32[1024]{0:T(1024)S(1)} %broadcast_multiply_fusion.2, f32[1024]{0:T(1024)S(1)} %copy-done.8, ...), kind=kOutput, calls=%fused_computation.35 | convolution fusion | flops 6473904128 | bytes 20996096 | tf_op jit(solution)/shard_map/dot_general | solution.py:275
  343.2 10.1 %all-reduce.6 = (bf16[1024]{0:T(1024)(128)(2,1)S(1)}, bf16[1024]{0:T(1024)(128)(2,1)S(1)}, bf16[3072]{0:T(1024)(128)(2,1)S(1)}, bf16[1024]{0:T(1024)(128)(2,1)S(1)}) all-reduce(bf16[1024]{0:T(1024)(128)(2,1)S(1)} %get-tuple-element.19, ...), channel_id=4, replica_groups=mesh['wide'=8,'narrow'=4] {'narrow'}, use_global_device_ids=true, to_apply=%region_8.9.clone | all-reduce | flops 6144 | bytes 24576
  353.3 0.1 dynamic-slice_convert_fusion.3
  353.4 0.1 dynamic-slice_convert_fusion.2
  353.4 0.1 dynamic-slice_convert_fusion.1
  353.5 0.1 dynamic-slice_convert_fusion
  353.6 210.0 %all-reduce.11 = (f32[256]{0:T(256)}, f32[256]{0:T(256)}, f32[1024,768]{1,0:T(8,128)}, f32[768]{0:T(1024)}, f32[256,1024]{1,0:T(8,128)}, /*index=5*/f32[1024]{0:T(1024)}, f32[256]{0:T(256)}) all-reduce(f32[256]{0:T(256)S(1)} %dynamic-slice_convert_fusion.3, ...), channel_id=1, replica_groups=mesh['wide'=8,'narrow'=4] {'wide'}, use_global_device_ids=true, to_apply=%region_9.10 | all-reduce | flops 1051136 | bytes 6311936 | tf_op jit(solution)/shard_map/psum | solution.py:396
  563.6 5.3 fusion.15
  568.9 7.3 fusion.20
  576.2 157.9 %all-reduce.10.cloned.1.call-done = (f32[1024,1024]{1,0:T(8,128)}, f32[1024,1024]{1,0:T(8,128)}) async-done(((f32[1024,1024]{1,0:T(8,128)}, f32[1024,1024]{1,0:T(8,128)}), (f32[1024,1024]{1,0:T(8,128)}, f32[1024,1024]{1,0:T(8,128)})) %all-reduce.10.cloned.1.call-update) | async-done | bytes 8388624 | tf_op jit(solution)/shard_map/psum | solution.py:396
  734.1 4.9 copy.34
  739.0 2.0 copy.35
  (51 shorter events, 0.2 us)
Async XLA Ops:
  7.2 152.3 %copy-start = (bf16[1024,1024]{1,0:T(8,128)(2,1)S(1)}, bf16[1024,1024]{1,0:T(8,128)(2,1)}, u32[]{:S(2)}) copy-start(bf16[1024,1024]{1,0:T(8,128)(2,1)} %param.21) | copy-start | bytes 6291460
  7.2 122.9 %all-gather.3.cloned.1.call-start = ((), (), s32[]{:S(2)}) async-start(), calls=%async_computation.4 | async-start | bytes 10485760 | tf_op jit(solution)/shard_map/all_gather | solution.py:330
  9.4 25.1 %copy-start.7 = (f32[1024]{0:T(1024)}, f32[1024]{0:T(1024)S(1)}, u32[]{:S(2)}) copy-start(f32[1024]{0:T(1024)S(1)} %convert_element_type.111) | copy-start | bytes 12292
  12.7 21.8 %copy-start.5 = (f32[1024,128]{1,0:T(8,128)}, f32[1024,128]{1,0:T(8,128)S(1)}, u32[]{:S(2)}) copy-start(f32[1024,128]{1,0:T(8,128)S(1)} %get-tuple-element.44.same_ref) | copy-start | bytes 1572868
  12.7 1.8 copy-start.1
  34.5 1.3 copy-start.3
  35.8 2.6 copy-start.9
  38.5 121.0 %all-gather.5.cloned.1.call-start = ((), (), s32[]{:S(2)}) async-start(), calls=%async_computation.6 | async-start | bytes 10485760 | tf_op jit(solution)/shard_map/all_gather | solution.py:352
  39.2 253.7 %reduce-scatter.11.cloned.1.call-start = ((), (), s32[]{:S(2)}) async-start(), calls=%async_computation.9 | async-start | bytes 2621440 | tf_op jit(solution)/shard_map/reduce_scatter | solution.py:382
  39.9 4.7 copy-start.6
  44.6 65.6 %copy-start.11 = (bf16[1024,1024]{1,0:T(8,128)(2,1)S(1)}, bf16[1024,1024]{1,0:T(8,128)(2,1)}, u32[]{:S(2)}) copy-start(bf16[1024,1024]{1,0:T(8,128)(2,1)} %param.23) | copy-start | bytes 6291460
  105.9 3.0 copy-start.2
  108.8 1.3 copy-start.10
  114.0 179.0 %reduce-scatter.9.cloned.1.call-start = ((), (), s32[]{:S(2)}) async-start(), calls=%async_computation.8 | async-start | bytes 7864320 | tf_op jit(solution)/shard_map/reduce_scatter | solution.py:376
  114.2 6.4 copy-start.4
  117.9 1.3 copy-start.12
  117.9 2.0 copy-start.13
  117.9 2.7 copy-start.14
  120.6 9.4 %copy-start.19 = (bf16[1024]{0:T(1024)(128)(2,1)S(1)}, bf16[1024]{0:T(1024)(128)(2,1)}, u32[]{:S(2)}) copy-start(bf16[1024]{0:T(1024)(128)(2,1)} %param.20) | copy-start | bytes 6148
  130.0 199.2 %reduce-scatter.7.cloned.1.call-start = ((), (), s32[]{:S(2)}) async-start(), calls=%async_computation.7 | async-start | bytes 10485760 | tf_op jit(solution)/shard_map/reduce_scatter | solution.py:361
  159.5 54.1 %copy-start.21 = (bf16[1024,1024]{1,0:T(8,128)(2,1)S(1)}, bf16[1024,1024]{1,0:T(8,128)(2,1)}, u32[]{:S(2)}) copy-start(bf16[1024,1024]{1,0:T(8,128)(2,1)} %param.19) | copy-start | bytes 6291460
  210.4 3.2 copy-start.23
  224.7 344.1 %reduce-scatter.5.cloned.1.call-start = ((), (), s32[]{:S(2)}) async-start(), calls=%async_computation.5 | async-start | bytes 10485760 | tf_op jit(solution)/shard_map/reduce_scatter | solution.py:339
  236.6 3.2 copy-start.15
  250.6 483.4 %all-reduce.10.cloned.1.call-start = ((), (), s32[]{:S(2)}) async-start(), calls=%async_computation.10 | async-start | bytes 16777216 | tf_op jit(solution)/shard_map/psum | solution.py:396
  250.7 15.9 %copy-start.16 = (bf16[4096,1024]{1,0:T(8,128)(2,1)S(1)}, bf16[4096,1024]{1,0:T(8,128)(2,1)}, u32[]{:S(2)}) copy-start(bf16[4096,1024]{1,0:T(8,128)(2,1)} %copy-done.15) | copy-start | bytes 25165828
  280.1 0.7 copy-start.22
  280.1 4.5 copy-start.20
  280.1 49.1 %copy-start.8 = (f32[1024]{0:T(1024)S(1)}, f32[1024]{0:T(1024)}, u32[]{:S(2)}) copy-start(f32[1024]{0:T(1024)} %copy-done.7) | copy-start | bytes 12292
  292.9 60.7 %copy-start.18 = (bf16[256,1024]{1,0:T(8,128)(2,1)S(1)}, bf16[256,1024]{1,0:T(8,128)(2,1)}, u32[]{:S(2)}) copy-start(bf16[256,1024]{1,0:T(8,128)(2,1)} %reduce-scatter.11.cloned.1.call-done) | copy-start | bytes 1572868
  734.1 4.9 copy-start.17
Sparse Core Ops, SparseCore 0:
  38.6 60.9 all-gather.2
  101.2 58.2 all-gather.4
  162.6 31.4 reduce-scatter.10
  196.6 58.3 reduce-scatter.8
  257.5 71.7 reduce-scatter.6
  331.8 71.6 reduce-scatter.4
  408.2 325.8 all-reduce.9

commit v2 on v1

--- a/solution.py
+++ b/solution.py
@@ -1,3 +1,4 @@
+import functools
 import math
 
 import jax
@@ -59,7 +60,7 @@
 
 
 def qkv_kernel(
-    x_ref, gain_ref, bias_ref, w_ref, b_ref, same_ref, down_ref, up_ref, out_ref, normed_ref
+    x_ref, gain_ref, bias_ref, w_ref, b_ref, same_ref, down_ref, up_ref, out_ref, normed_ref, turned_ref
 ):
     step = pl.program_id(0)
     rows, cols = out_ref.shape
@@ -73,9 +74,9 @@
             centered = x - mean
             variance = jnp.mean(centered * centered, axis=-1, keepdims=True)
             unit = centered * lax.rsqrt(variance + 1e-05)
-            normed_ref[r : r + TILE, :] = (unit * gain_ref[...] + bias_ref[...]).astype(
-                jnp.bfloat16
-            )
+            normed = unit * gain_ref[...] + bias_ref[...]
+            normed_ref[r : r + TILE, :] = normed.astype(jnp.bfloat16)
+            turned_ref[:, r : r + TILE] = normed.T.astype(jnp.bfloat16)
 
     scale = jnp.where(step < blocks, 1.0 / math.sqrt(HEAD), 1.0)
     for r in range(0, rows, TILE):
@@ -113,12 +114,13 @@
             whole((rows, PAIR)),
             whole((rows, PAIR)),
         ],
-        out_specs=[pl.BlockSpec((rows, cols), lambda j: (0, j)), whole((rows, width))],
+        out_specs=[pl.BlockSpec((rows, cols), lambda j: (0, j)), whole((rows, width)), whole((width, rows))],
         out_shape=[
             jax.ShapeDtypeStruct((rows, w_qkv.shape[1]), jnp.bfloat16),
             jax.ShapeDtypeStruct((rows, width), jnp.bfloat16),
+            jax.ShapeDtypeStruct((width, rows), jnp.bfloat16),
         ],
-        compiler_params=pltpu.CompilerParams(vmem_limit_bytes=40 << 20),
+        compiler_params=pltpu.CompilerParams(vmem_limit_bytes=60 << 20),
         cost_estimate=pl.CostEstimate(
             flops=2 * rows * width * w_qkv.shape[1],
             bytes_accessed=2 * (rows * width * 2 + width * w_qkv.shape[1] * 2),
@@ -258,159 +260,767 @@
             jax.ShapeDtypeStruct((rows, width), jnp.bfloat16),
             jax.ShapeDtypeStruct((3, rows, width), jnp.bfloat16),
         ],
-        compiler_params=pltpu.CompilerParams(vmem_limit_bytes=40 << 20),
+        compiler_params=pltpu.CompilerParams(vmem_limit_bytes=60 << 20),
         cost_estimate=pl.CostEstimate(
             flops=16 * rows * rows * width, bytes_accessed=16 * rows * width, transcendentals=0
         ),
     )(first, starts[None, :], qkv, qkv, qkv, grad_att, *coefs)
 
 
-def contract_rows(left, right):
-    return lax.dot_general(
-        left, right, (((0,), (0,)), ((), ())), preferred_element_type=jnp.float32
-    )
-
-
-def contract_cols(left, right):
-    return lax.dot_general(
-        left, right, (((1,), (1,)), ((), ())), preferred_element_type=jnp.float32
-    )
-
-
-def exact_gelu(values_in):
-    return jax.nn.gelu(values_in, approximate=False)
-
-
-def body(
+CORE, YAXIS, XHALF, NEAR, BACK, WIDE_A, WIDE_B, FAR = range(8)
+BLOCKS, QKV, DENSE = 12, 3, 3
+F_RING, Y_RING, S_RING = 8, 4, 2
+PACK = 2 * TILE + 16
+LAGS = (2, 3, 4, 5, 6, 7)
+MESH = pl.DeviceIdType.MESH
+
+
+def xor2(value, other):
+    return (value + other) % 2 + 2 * ((value // 2 + other // 2) % 2)
+
+
+def gelu_parts(x):
+    cdf = 0.5 * (1.0 + lax.erf(x * math.sqrt(0.5)))
+    density = jnp.exp(-0.5 * x * x) * (1.0 / math.sqrt(2.0 * math.pi))
+    return x * cdf, cdf + x * density
+
+
+def widen(value):
+    return value.astype(jnp.float32)
+
+
+def main_kernel(
+    wide,
     tokens,
-    seg_ids,
-    ln_gain,
-    ln_bias,
+    normed,
+    normed_t,
+    cot,
+    attended,
+    gp,
     w_qkv,
-    b_qkv,
     w_dense,
-    w_up,
-    b_up,
-    w_down,
+    own_w,
+    y_w,
+    gain,
     out_bias,
-    cotangent,
+    mixed_out,
+    dtok_out,
+    straight_out,
+    turned_out,
+    small_out,
+    core_w,
+    diag_w,
+    nrm,
+    nrm_t,
+    ct,
+    ct_t,
+    hid,
+    gpre,
+    pool,
+    mixed_acc,
+    gn_acc,
+    slope,
+    s_ring,
+    a_ring,
+    f_ring,
+    r_ring,
+    ry,
+    rx,
+    rz,
+    rfar,
+    gz,
+    gx,
+    tbuf,
+    bias,
+    sv,
+    sv_sum,
+    sv_recv,
+    send,
+    recv,
+    far_send,
+    far_recv,
+    sv_send,
+    sv_rsem,
+    load,
+    load_w,
+    out_sem,
+    w_send,
+    w_recv,
+    free,
+    y_free,
 ):
-    tok_rows, model_width = tokens.shape
-    seq_count, seq_len = seg_ids.shape
-    tok_f32 = tokens.astype(jnp.float32)
-    row_mean = jnp.mean(tok_f32, axis=-1, keepdims=True)
-    centered = tok_f32 - row_mean
-    variance = jnp.mean(centered * centered, axis=-1, keepdims=True)
-    inv_std = lax.rsqrt(variance + 1e-05)
-    unit_rows = centered * inv_std
-    gain_f32 = ln_gain.astype(jnp.float32)
-    starts = doc_starts(seg_ids)
-    position = jnp.arange(seq_len, dtype=jnp.int32)[None, :] - starts
-    grad_att = contract_cols(cotangent, w_dense).astype(jnp.bfloat16)
-    pieces = []
-    for s in range(seq_count):
-        part = slice(s * seq_len, (s + 1) * seq_len)
-        coefs = rope_coefs(position[s])
-        qkv, normed_part = project(
-            tokens[part],
-            gain_f32[None, :],
+    rows = nrm.shape[0]
+    R_RING, A_RING = r_ring.shape[1], a_ring.shape[0]
+    n, w = lax.axis_index("narrow"), lax.axis_index("wide")
+    near = w % 4
+    xbit, zbit = w % 2, (w // 2) % 2
+    bits = [b for b in range(2, 20) if (1 << b) < wide]
+    mate = {"narrow": n + 1 - 2 * (n % 2)}
+    ymate = {"narrow": n + 2 - 4 * (n // 2)}
+
+    def across(bit):
+        return {"wide": w + (1 << bit) - (2 << bit) * ((w // (1 << bit)) % 2)}
+
+    def spot(r):
+        return xor2(n, r)
+
+    partners = [mate, ymate] + [across(b) for b in [0, 1] + bits]
+    barrier = pltpu.get_barrier_semaphore()
+    for p in partners:
+        pl.semaphore_signal(barrier, inc=1, device_id=p, device_id_type=MESH)
+    pl.semaphore_wait(barrier, len(partners))
+
+    half, quarter = rows // 2, rows // 4
+    own_half, other_half = half * xbit, half * (1 - xbit)
+    own_q = own_half + quarter * zbit
+    other_q = own_half + quarter * (1 - zbit)
+
+    def seg(start, size):
+        return pl.ds(pl.multiple_of(start, quarter), size)
+
+    def remote(src, dst, kind, b, dev):
+        return pltpu.make_async_remote_copy(
+            src_ref=src,
+            dst_ref=dst,
+            send_sem=send.at[kind, b],
+            recv_sem=recv.at[kind, b],
+            device_id=dev,
+            device_id_type=MESH,
+        )
+
+    def core_copy(which, b):
+        return remote(
+            s_ring.at[which, b % S_RING],
+            r_ring.at[which, b % R_RING],
+            CORE if which == 0 else BACK,
+            b,
+            mate,
+        )
+
+    def y_copy(b):
+        return remote(a_ring.at[b % A_RING], ry.at[b % Y_RING], YAXIS, b, ymate)
+
+    def x_copy(b):
+        return remote(f_ring.at[b % F_RING, seg(other_half, half)], rx.at[b], XHALF, b, across(0))
+
+    def z_copy(b):
+        return remote(f_ring.at[b % F_RING, seg(other_q, quarter)], rz.at[b], NEAR, b, across(1))
+
+    def far_copy(i, b):
+        return pltpu.make_async_remote_copy(
+            src_ref=f_ring.at[b % F_RING, seg(own_q, quarter)],
+            dst_ref=rfar.at[i, b],
+            send_sem=far_send.at[i, b],
+            recv_sem=far_recv.at[i, b],
+            device_id=across(bits[i]),
+            device_id_type=MESH,
+        )
+
+    def back_z(b):
+        return remote(f_ring.at[b % F_RING, seg(own_q, quarter)], gz.at[b], FAR, b, across(1))
+
+    def back_xa(b):
+        return remote(
+            f_ring.at[b % F_RING, seg(own_q, quarter)], gx.at[b, 0], WIDE_A, b, across(0)
+        )
+
+    def back_xb(b):
+        return remote(gz.at[b], gx.at[b, 1], WIDE_B, b, across(0))
+
+    def is_turned(b):
+        return (b == DENSE) | ((b > DENSE) & (b % 2 == 0))
+
+    def piece(i, b):
+        src = (
+            f_ring.at[b % F_RING, seg(own_q, quarter)],
+            gz.at[b],
+            gx.at[b, 0],
+            gx.at[b, 1],
+        )[i]
+        at = own_half if i < 2 else other_half
+        return src, at + quarter * (zbit if i % 2 == 0 else 1 - zbit)
+
+    def straight_copy(i, b):
+        src, at = piece(i, b)
+        column = jnp.where(b < QKV, b, QKV + (b - DENSE - 2) // 2)
+        column = pl.ds(pl.multiple_of(column * TILE, TILE), TILE)
+        return pltpu.make_async_copy(
+            src, straight_out.at[seg(at, quarter), column], out_sem.at[i, b]
+        )
+
+    def turned_copy(i, b):
+        src, at = piece(i, b)
+        row = jnp.where(b == DENSE, 0, 1 + (b - DENSE - 1) // 2)
+        return pltpu.make_async_copy(
+            tbuf.at[(b // 2) % 2, i],
+            turned_out.at[pl.ds(pl.multiple_of(row * TILE, TILE), TILE), seg(at, quarter)],
+            out_sem.at[i, b],
+        )
+
+    def put(i, b):
+        @pl.when(is_turned(b))
+        def _():
+            src, at = piece(i, b)
+            tbuf[(b // 2) % 2, i] = widen(src[...]).T.astype(jnp.bfloat16)
+            turned_copy(i, b).start()
+
+        @pl.when(jnp.logical_not(is_turned(b)))
+        def _():
+            straight_copy(i, b).start()
+
+    def add_into(b, start, size, other):
+        at = seg(start, size)
+        slot = b % F_RING
+        f_ring[slot, at] = (widen(f_ring[slot, at]) + widen(other[...])).astype(jnp.bfloat16)
+
+    def stage_y(b):
+        y_copy(b).wait_recv()
+        add_into(b, other_half, half, ry.at[b % Y_RING, seg(other_half, half)])
+        x_copy(b).start()
+        add_into(b, own_half, half, ry.at[b % Y_RING, seg(own_half, half)])
+
+        @pl.when(b + Y_RING < BLOCKS)
+        def _():
+            pl.semaphore_signal(y_free, inc=1, device_id=ymate, device_id_type=MESH)
+
+    def stage_x(b):
+        x_copy(b).wait_recv()
+        add_into(b, other_q, quarter, rx.at[b, seg(quarter * (1 - zbit), quarter)])
+        z_copy(b).start()
+        add_into(b, own_q, quarter, rx.at[b, seg(quarter * zbit, quarter)])
+
+    def stage_near(b):
+        z_copy(b).wait_recv()
+        add_into(b, own_q, quarter, rz.at[b])
+        far_copy(0, b).start()
+
+    def stage_far(b):
+        for i in range(len(bits)):
+            far_copy(i, b).wait()
+            add_into(b, own_q, quarter, rfar.at[i, b])
+            if i + 1 < len(bits):
+                far_copy(i + 1, b).start()
+        back_z(b).start()
+        back_xa(b).start()
+        put(0, b)
+        x_copy(b).wait_send()
+        z_copy(b).wait_send()
+
+    def stage_back(b):
+        back_z(b).wait_recv()
+        back_xb(b).start()
+        put(1, b)
+
+    def stage_out(b):
+        back_xa(b).wait_recv()
+        put(2, b)
+        back_xb(b).wait_recv()
+        put(3, b)
+        back_z(b).wait_send()
+        back_xa(b).wait_send()
+        back_xb(b).wait_send()
+        for i in range(4):
+            straight_copy(i, b).wait()
+
+    stages = (stage_y, stage_x, stage_near, stage_far, stage_back, stage_out)
+
+    def progress(t):
+        for lag, stage in reversed(list(zip(LAGS, stages))):
+            b = t - lag
+
+            @pl.when((b >= 0) & (b < BLOCKS))
+            def _(stage=stage, b=b):
+                stage(b)
+
+    step = rows // 2
+
+    def tile(r, b, left, right):
+        if r in (1, 3):
+            which = r // 2
+
+            @pl.when(b >= S_RING)
+            def _():
+                core_copy(which, b - S_RING).wait_send()
+
+            def chunk(m, c):
+                at = pl.ds(pl.multiple_of(m * step, step), step)
+                s_ring[which, b % S_RING, at] = dot_nn(left[at, :], right[...]).astype(jnp.bfloat16)
+                return c
+
+            lax.fori_loop(0, 2, chunk, 0)
+            if which == 0:
+
+                @pl.when(b >= R_RING)
+                def _():
+                    pl.semaphore_wait(free, 1)
+
+            core_copy(which, b).start()
+        else:
+            which = 1 if r == 2 else 0
+            if r == 2:
+
+                @pl.when(b >= A_RING)
+                def _():
+                    y_copy(b - A_RING).wait_send()
+
+            core_copy(which, b).wait_recv()
+            target = a_ring.at[b % A_RING] if r == 2 else f_ring.at[b % F_RING]
+
+            def chunk(m, c):
+                at = pl.ds(pl.multiple_of(m * step, step), step)
+                target[at] = (
+                    dot_nn(left[at, :], right[...]) + widen(r_ring[which, b % R_RING, at])
+                ).astype(jnp.bfloat16)
+                return c
+
+            lax.fori_loop(0, 2, chunk, 0)
+            if r == 2:
+
+                @pl.when(b >= Y_RING)
+                def _():
+                    pl.semaphore_wait(y_free, 1)
+
+                y_copy(b).start()
+            else:
+
+                @pl.when(b + R_RING < BLOCKS)
+                def _():
+                    pl.semaphore_signal(free, inc=1, device_id=mate, device_id_type=MESH)
+
+    def accumulate(target, left, right, transposed, first):
+        size = rows // 4
+
+        def chunk(m, c):
+            at = pl.ds(pl.multiple_of(m * size, size), size)
+            dot = dot_nt if transposed else dot_nn
+            got = dot(left[at, :], right[...])
+            target[at, :] = got if first else target[at, :] + got
+            return c
+
+        lax.fori_loop(0, 4, chunk, 0)
+
+    def weight_copy(k, at):
+        return pltpu.make_async_remote_copy(
+            src_ref=(own_w, y_w)[k].at[at],
+            dst_ref=(core_w, diag_w)[k].at[at],
+            send_sem=w_send.at[k, at],
+            recv_sem=w_recv.at[k, at],
+            device_id=mate,
+            device_id_type=MESH,
+        )
+
+    firsts = [
+        pltpu.make_async_copy(normed_t, nrm_t, load.at[0]),
+        pltpu.make_async_copy(cot, ct, load.at[1]),
+        pltpu.make_async_copy(attended, hid, load.at[2]),
+        pltpu.make_async_copy(w_dense, gpre, load.at[3]),
+        pltpu.make_async_copy(normed, nrm, load.at[4]),
+    ]
+    firsts[0].start()
+
+    def gp_tile(r, j):
+        at = 3 * spot(r) + j
+        return pltpu.make_async_copy(
+            gp.at[at // 4, :, pl.ds(pl.multiple_of((at % 4) * TILE, TILE), TILE)],
+            pool.at[j % 2, :, r * TILE : (r + 1) * TILE],
+            load_w.at[j % 2, r],
+        )
+
+    def chunk_copies(c):
+        return [
+            pltpu.make_async_copy(gp.at[c], pool.at[2], load.at[6]),
+            pltpu.make_async_copy(
+                w_qkv.at[:, pl.ds(pl.multiple_of(c * rows, rows), rows)], pool.at[3], load.at[7]
+            ),
+        ]
+
+    for r in (1, 3, 2, 0):
+        gp_tile(r, 0).start()
+    for c in firsts[1:]:
+        c.start()
+    for c in chunk_copies(0):
+        c.start()
+    sv[...] = jnp.zeros_like(sv)
+    firsts[0].wait()
+
+    def qkv_block(j, carry):
+        @pl.when(j + 1 < QKV)
+        def _():
+            for r in (1, 3, 2, 0):
+                gp_tile(r, j + 1).start()
+
+        for r in (1, 3, 2, 0):
+            gp_tile(r, j).wait()
+            mine = pool.at[j % 2, :, r * TILE : (r + 1) * TILE]
+            tile(r, j, nrm_t, mine)
+            sv[r, pl.ds(3 + j, 1), :] = jnp.sum(widen(mine[...]), axis=0, keepdims=True)
+
+        @pl.when(j == 0)
+        def _():
+            for at in range(4):
+                weight_copy(0, at).start()
+                weight_copy(1, at).start()
+            firsts[1].wait()
+            for at in range(0, rows, TILE):
+                ct_t[:, at : at + TILE] = widen(ct[at : at + TILE, :]).T.astype(jnp.bfloat16)
+
+        for c in chunk_copies(j):
+            c.wait()
+
+        @pl.when(j == 0)
+        def _():
+            accumulate(gn_acc, pool.at[2], pool.at[3], True, True)
+
+        @pl.when(j > 0)
+        def _():
+            accumulate(gn_acc, pool.at[2], pool.at[3], True, False)
+
+        @pl.when(j + 1 < QKV)
+        def _():
+            for c in chunk_copies(j + 1):
+                c.start()
+
+        progress(j)
+        return carry
+
+    lax.fori_loop(0, QKV, qkv_block, 0)
+
+    for c in firsts[2:]:
+        c.wait()
+    for r in (1, 3, 2, 0):
+        at = pl.ds(pl.multiple_of(spot(r) * TILE, TILE), TILE)
+        tile(r, DENSE, ct_t, hid.at[:, at])
+    accumulate(mixed_acc, hid, gpre, False, True)
+    progress(DENSE)
+
+    def weights(cb):
+        slot = cb % 2
+        far = xor2(cb, near)
+        copies = []
+        for r, src in enumerate((own_w.at[cb], core_w.at[cb], y_w.at[far], diag_w.at[far])):
+            copies.append(
+                pltpu.make_async_copy(
+                    src.at[2 * TILE : PACK], bias.at[slot, r], load_w.at[2 + slot, 8 + r]
+                )
+            )
+            for k in range(2):
+                copies.append(
+                    pltpu.make_async_copy(
+                        src.at[k * TILE : (k + 1) * TILE],
+                        pool.at[2 * slot + k, r * TILE : (r + 1) * TILE],
+                        load_w.at[2 + slot, 2 * r + k],
+                    )
+                )
+        return copies
+
+    def weights_here(cb):
+        weight_copy(0, cb).wait_recv()
+        weight_copy(1, xor2(cb, near)).wait_recv()
+        for c in weights(cb):
+            c.start()
+
+    weights_here(0)
+
+    def mlp_block(cb, carry):
+        slot = cb % 2
+
+        @pl.when(cb < 3)
+        def _():
+            weights_here(cb + 1)
+
+        for c in weights(cb):
+            c.wait()
+        for r in (1, 3, 2, 0):
+            cols = slice(r * TILE, (r + 1) * TILE)
+            up, down = pool.at[2 * slot, cols], pool.at[2 * slot + 1, cols]
+
+            bias_row = widen(bias[slot, r, 0:1, 0:TILE])
+
+            def act(m, c):
+                at = pl.ds(pl.multiple_of(m * TILE, TILE), TILE)
+                pre = dot_nt(nrm[at, :], up[...]) + bias_row
+                value, grad = gelu_parts(pre)
+                hid[at, cols] = value.astype(jnp.bfloat16)
+                slope[at, :] = grad
+                return c
+
+            lax.fori_loop(0, rows // TILE, act, 0)
+            tile(r, 4 + 2 * cb, ct_t, hid.at[:, cols])
+
+            def back(m, total):
+                at = pl.ds(pl.multiple_of(m * TILE, TILE), TILE)
+                low = (dot_nt(ct[at, :], down[...]) * slope[at, :]).astype(jnp.bfloat16)
+                gpre[at, cols] = low
+                return total + jnp.sum(widen(low), axis=0, keepdims=True)
+
+            total = lax.fori_loop(0, rows // TILE, back, jnp.zeros((1, TILE), jnp.float32))
+            sv[r, pl.ds(6 + cb, 1), :] = total
+            if r == 0:
+                progress(4 + 2 * cb)
+            tile(r, 5 + 2 * cb, nrm_t, gpre.at[:, cols])
+        accumulate(mixed_acc, hid, pool.at[2 * slot + 1], False, False)
+        accumulate(gn_acc, gpre, pool.at[2 * slot], False, False)
+        progress(5 + 2 * cb)
+        return carry
+
+    lax.fori_loop(0, 4, mlp_block, 0)
+
+    tok_load = pltpu.make_async_copy(tokens, pool.at[0], load.at[0])
+    tok_load.start()
+    progress(BLOCKS)
+    tok_load.wait()
+
+    def finish(m, sums):
+        at = pl.ds(pl.multiple_of(m * TILE, TILE), TILE)
+        x = widen(pool[0, at, :])
+        mean = jnp.mean(x, axis=-1, keepdims=True)
+        centered = x - mean
+        variance = jnp.mean(centered * centered, axis=-1, keepdims=True)
+        inv_std = lax.rsqrt(variance + 1e-05)
+        unit = centered * inv_std
+        hid[at, :] = (mixed_acc[at, :] + x + out_bias[...]).astype(jnp.bfloat16)
+        gn = gn_acc[at, :]
+        g = gn * gain[...]
+        mean_grad = jnp.mean(g, axis=-1, keepdims=True)
+        mean_proj = jnp.mean(g * unit, axis=-1, keepdims=True)
+        c = widen(ct[at, :])
+        gpre[at, :] = (c + inv_std * (g - mean_grad - unit * mean_proj)).astype(jnp.bfloat16)
+        return (
+            sums[0] + jnp.sum(gn * unit, axis=0, keepdims=True),
+            sums[1] + jnp.sum(gn, axis=0, keepdims=True),
+            sums[2] + jnp.sum(c, axis=0, keepdims=True),
+        )
+
+    zero = jnp.zeros((1, rows), jnp.float32)
+    sums = lax.fori_loop(0, rows // TILE, finish, (zero, zero, zero))
+    final = [
+        pltpu.make_async_copy(hid, mixed_out, load.at[1]),
+        pltpu.make_async_copy(gpre, dtok_out, load.at[2]),
+    ]
+    for c in final:
+        c.start()
+    for i in range(3):
+        sv_sum[i : i + 1, :] = sums[i]
+    for r in range(4):
+        at = pl.ds(pl.multiple_of(spot(r) * TILE, TILE), TILE)
+        sv[r, 0:3, :] = sv_sum[0:3, at]
+
+    def sv_copy(i, src, dev):
+        return pltpu.make_async_remote_copy(
+            src_ref=src,
+            dst_ref=sv_recv.at[i],
+            send_sem=sv_send.at[i],
+            recv_sem=sv_rsem.at[i],
+            device_id=dev,
+            device_id_type=MESH,
+        )
+
+    hops = [
+        sv_copy(0, sv.at[1], mate),
+        sv_copy(1, sv.at[3], mate),
+        sv_copy(2, sv.at[2], ymate),
+    ]
+    hops += [sv_copy(3 + i, sv.at[0], across(b)) for i, b in enumerate([0, 1] + bits)]
+    hops[0].start()
+    hops[1].start()
+    progress(BLOCKS + 1)
+    hops[0].wait()
+    hops[1].wait()
+    sv[0] = sv[0] + sv_recv[0]
+    sv[2] = sv[2] + sv_recv[1]
+    hops[2].start()
+    progress(BLOCKS + 2)
+    hops[2].wait()
+    sv[0] = sv[0] + sv_recv[2]
+    for i in range(3, len(hops)):
+        hops[i].start()
+        if i < 6:
+            progress(BLOCKS + i)
+        hops[i].wait()
+        sv[0] = sv[0] + sv_recv[i]
+    for i in range(len(hops), 6):
+        progress(BLOCKS + i)
+    small_out[...] = sv[0]
+    progress(BLOCKS + 6)
+
+    for at in range(4):
+        weight_copy(0, at).wait_send()
+        weight_copy(1, at).wait_send()
+    for c in final:
+        c.wait()
+    for b in range(BLOCKS - S_RING, BLOCKS):
+        core_copy(0, b).wait_send()
+        core_copy(1, b).wait_send()
+    for b in range(BLOCKS - A_RING, BLOCKS):
+        y_copy(b).wait_send()
+
+
+def main_call(wide, hbm_args, vmem_args):
+    tokens = hbm_args[0]
+    rows, width = tokens.shape
+    hops = max(wide.bit_length() - 1, 2)
+    far = hops - 2
+    bf, f32 = jnp.bfloat16, jnp.float32
+    half, quarter = rows // 2, rows // 4
+    vm = pltpu.VMEM
+    dma = pltpu.SemaphoreType.DMA
+    return pl.pallas_call(
+        functools.partial(main_kernel, wide),
+        in_specs=[pl.BlockSpec(memory_space=pl.ANY)] * len(hbm_args)
+        + [pl.BlockSpec(memory_space=pltpu.VMEM)] * len(vmem_args),
+        out_specs=[pl.BlockSpec(memory_space=pl.ANY)] * 4
+        + [pl.BlockSpec(memory_space=pltpu.VMEM)]
+        + [pl.BlockSpec(memory_space=pl.ANY)] * 2,
+        out_shape=[
+            jax.ShapeDtypeStruct((rows, width), bf),
+            jax.ShapeDtypeStruct((rows, width), bf),
+            jax.ShapeDtypeStruct((width, 7 * TILE), bf),
+            jax.ShapeDtypeStruct((5 * TILE, width), bf),
+            jax.ShapeDtypeStruct((16, TILE), f32),
+            jax.ShapeDtypeStruct((4, PACK, width), bf),
+            jax.ShapeDtypeStruct((4, PACK, width), bf),
+        ],
+        scratch_shapes=[
+            vm((rows, width), bf),
+            vm((width, rows), bf),
+            vm((rows, width), bf),
+            vm((width, rows), bf),
+            vm((rows, width), bf),
+            vm((rows, width), bf),
+            vm((4, rows, width), bf),
+            vm((rows, width), f32),
+            vm((rows, width), f32),
+            vm((rows, TILE), f32),
+            vm((2, S_RING, width, TILE), bf),
+            vm((4 if far < 2 else 2, width, TILE), bf),
+            vm((F_RING, width, TILE), bf),
+            vm((2, 4 if far < 2 else 2, width, TILE), bf),
+            vm((Y_RING, width, TILE), bf),
+            vm((BLOCKS, half, TILE), bf),
+            vm((BLOCKS, quarter, TILE), bf),
+            vm((far, BLOCKS, quarter, TILE), bf),
+            vm((BLOCKS, quarter, TILE), bf),
+            vm((BLOCKS, 2, quarter, TILE), bf),
+            vm((2, 4, TILE, TILE), bf),
+            vm((2, 4, 16, width), bf),
+            vm((4, 16, TILE), f32),
+            vm((8, width), f32),
+            vm((3 + hops, 16, TILE), f32),
+            dma((8, BLOCKS)),
+            dma((8, BLOCKS)),
+            dma((far, BLOCKS)),
+            dma((far, BLOCKS)),
+            dma((3 + hops,)),
+            dma((3 + hops,)),
+            dma((8,)),
+            dma((4, 12)),
+            dma((4, BLOCKS)),
+            dma((2, 4)),
+            dma((2, 4)),
+            pltpu.SemaphoreType.REGULAR,
+            pltpu.SemaphoreType.REGULAR,
+        ],
+        compiler_params=pltpu.CompilerParams(
+            collective_id=0, has_side_effects=True, vmem_limit_bytes=61 << 20
+        ),
+        cost_estimate=pl.CostEstimate(
+            flops=70 * rows * width * width, bytes_accessed=80 << 20, transcendentals=0
+        ),
+    )(*hbm_args, *vmem_args)
+
+
+def flip(value, axis, bit, size):
+    return lax.ppermute(value, axis, [(i, i ^ bit) for i in range(size)])
+
+
+def make_body(wide):
+    def body(
+        tokens,
+        seg_ids,
+        ln_gain,
+        ln_bias,
+        w_qkv,
+        b_qkv,
+        w_dense,
+        w_up,
+        b_up,
+        w_down,
+        out_bias,
+        cotangent,
+    ):
+        seq_len = seg_ids.shape[1]
+        width = tokens.shape[1]
+        index = lax.axis_index("wide")
+        near = index % 4
+
+        pad = jnp.zeros((4, 16, width - TILE), jnp.bfloat16)
+        b_rows = jnp.broadcast_to(b_up.reshape(4, 1, TILE), (4, 16, TILE))
+        own_w = jnp.concatenate(
+            [
+                w_up.T.reshape(4, TILE, width),
+                w_down.reshape(4, TILE, width),
+                jnp.concatenate([b_rows, pad], axis=2),
+            ],
+            axis=1,
+        )
+        across_y = flip(
+            lax.dynamic_index_in_dim(own_w, near, 0, keepdims=False), "narrow", 2, 4
+        )
+
+        starts = doc_starts(seg_ids)
+        position = jnp.arange(seq_len, dtype=jnp.int32)[None, :] - starts
+        coefs = rope_coefs(position[0])
+        gain = ln_gain.astype(jnp.float32)[None, :]
+        grad_att = dot_nt(cotangent, w_dense).astype(jnp.bfloat16)
+        qkv, normed, normed_t = project(
+            tokens,
+            gain,
             ln_bias.astype(jnp.float32)[None, :],
             w_qkv,
             b_qkv.astype(jnp.float32)[None, :],
             coefs,
         )
-        att_part, grad_part = attend(qkv, grad_att[part], starts[s], coefs)
-        pieces.append((normed_part, att_part, grad_part))
-    normed_low, attended_low = (
-        jnp.concatenate([p[i] for p in pieces], axis=0) for i in range(2)
-    )
-    grad_proj = jnp.concatenate([p[2] for p in pieces], axis=1)
-    grad_proj = jnp.concatenate([grad_proj[i] for i in range(3)], axis=1)
-    attn_out = jnp.dot(attended_low, w_dense, preferred_element_type=jnp.float32)
-    normed_all = lax.all_gather(normed_low, "narrow", axis=0, tiled=True)
-    pre_act = jnp.dot(normed_all, w_up, preferred_element_type=jnp.float32) + b_up.astype(
-        jnp.float32
-    )
-    hidden = exact_gelu(pre_act).astype(jnp.bfloat16)
-    row_piece = hidden
-    partial_low = jnp.dot(row_piece, w_down, preferred_element_type=jnp.float32).astype(
-        jnp.bfloat16
-    )
-    mlp_out = lax.psum_scatter(
-        lax.optimization_barrier(partial_low).astype(jnp.float32).astype(jnp.bfloat16),
-        "narrow",
-        scatter_dimension=0,
-        tiled=True,
-    ).astype(jnp.float32)
-    mixed = (tok_f32 + attn_out + mlp_out + out_bias.astype(jnp.float32)).astype(jnp.bfloat16)
-    grad_f32 = cotangent.astype(jnp.float32)
-    d_out_bias = jnp.sum(grad_f32, axis=0)
-    d_w_dense = contract_rows(attended_low, cotangent)
-    d_w_qkv = contract_rows(normed_low, grad_proj)
-    d_b_qkv = jnp.sum(grad_proj.astype(jnp.float32), axis=0)
-    grad_normed = contract_cols(grad_proj, w_qkv)
-    grad_all = lax.all_gather(cotangent, "narrow", axis=0, tiled=True)
-    grad_hidden = contract_cols(grad_all, w_down)
-    unused, gelu_pull = jax.vjp(exact_gelu, pre_act)
-    grad_pre = gelu_pull(grad_hidden)[0].astype(jnp.bfloat16)
-    d_w_down = contract_rows(hidden, grad_all)
-    d_w_up = contract_rows(normed_all, grad_pre)
-    d_b_up = jnp.sum(grad_pre.astype(jnp.float32), axis=0)
-    row_piece = grad_pre
-    partial_low = contract_cols(row_piece, w_up).astype(jnp.bfloat16)
-    grad_normed = grad_normed + lax.psum_scatter(
-        lax.optimization_barrier(partial_low).astype(jnp.float32).astype(jnp.bfloat16),
-        "narrow",
-        scatter_dimension=0,
-        tiled=True,
-    ).astype(jnp.float32)
-    grad_unit = grad_normed * gain_f32
-    d_ln_gain = jnp.sum(grad_normed * unit_rows, axis=0)
-    d_ln_bias = jnp.sum(grad_normed, axis=0)
-    mean_grad = jnp.mean(grad_unit, axis=-1, keepdims=True)
-    mean_proj = jnp.mean(grad_unit * unit_rows, axis=-1, keepdims=True)
-    d_tokens = (grad_f32 + inv_std * (grad_unit - mean_grad - unit_rows * mean_proj)).astype(
-        jnp.bfloat16
-    )
-    shares = (
-        lax.psum_scatter(
-            d_w_qkv.astype(jnp.bfloat16), "narrow", scatter_dimension=1, tiled=True
-        ).astype(jnp.float32),
-        lax.psum_scatter(
-            d_b_qkv.astype(jnp.bfloat16), "narrow", scatter_dimension=0, tiled=True
-        ).astype(jnp.float32),
-        lax.psum_scatter(
-            d_w_dense.astype(jnp.bfloat16), "narrow", scatter_dimension=0, tiled=True
-        ).astype(jnp.float32),
-        lax.psum_scatter(
-            d_out_bias.astype(jnp.bfloat16), "narrow", scatter_dimension=0, tiled=True
-        ).astype(jnp.float32),
-        lax.psum_scatter(
-            d_ln_gain.astype(jnp.bfloat16), "narrow", scatter_dimension=0, tiled=True
-        ).astype(jnp.float32),
-        lax.psum_scatter(
-            d_ln_bias.astype(jnp.bfloat16), "narrow", scatter_dimension=0, tiled=True
-        ).astype(jnp.float32),
-    )
-    d_w_qkv, d_b_qkv, d_w_dense, d_out_bias, d_ln_gain, d_ln_bias = shares
-    summed = lax.psum(
-        (d_w_qkv, d_b_qkv, d_w_dense, d_out_bias, d_ln_gain, d_ln_bias, d_w_up, d_b_up, d_w_down),
-        "wide",
-    )
-    d_w_qkv, d_b_qkv, d_w_dense, d_out_bias, d_ln_gain, d_ln_bias, d_w_up, d_b_up, d_w_down = summed
-    return (
-        mixed,
-        d_tokens,
-        d_ln_gain,
-        d_ln_bias,
-        d_w_qkv,
-        d_b_qkv,
-        d_w_dense,
-        d_w_up,
-        d_b_up,
-        d_w_down,
-        d_out_bias,
-    )
+        across_y, qkv, grad_att = lax.optimization_barrier((across_y, qkv, grad_att))
+        others = [flip(across_y, "wide", k, wide) for k in (1, 2, 3)]
+        attended, grad_proj = attend(qkv, grad_att, starts[0], coefs)
+        others, attended = lax.optimization_barrier((others, attended))
+        y_w = jnp.stack([across_y] + others, axis=0)
+        mixed, d_tokens, straight, turned, small, _, _ = main_call(
+            wide,
+            (
+                tokens,
+                normed,
+                normed_t,
+                cotangent,
+                attended,
+                grad_proj,
+                w_qkv,
+                w_dense,
+                own_w,
+                y_w,
+            ),
+            (gain, out_bias.astype(jnp.float32)[None, :]),
+        )
+        q = QKV * TILE
+        d_w_qkv = straight[:, :q].astype(jnp.float32)
+        d_w_up = straight[:, q:].astype(jnp.float32)
+        d_w_dense = turned[:TILE].astype(jnp.float32)
+        d_w_down = turned[TILE:].astype(jnp.float32)
+        return (
+            mixed,
+            d_tokens,
+            small[0],
+            small[1],
+            d_w_qkv,
+            small[3:6].reshape(-1),
+            d_w_dense,
+            d_w_up,
+            small[6:10].reshape(-1),
+            d_w_down,
+            small[2],
+        )
+
+    return body
 
 
 def solution(mesh):
@@ -441,4 +1051,5 @@
         P("narrow", None),
         P("narrow"),
     )
-    return jax.shard_map(body, mesh=mesh, in_specs=in_specs, out_specs=out_specs, check_vma=False)
+    return jax.shard_map(
+        make_body(mesh.shape["wide"]), mesh=mesh, in_specs=in_specs, out_specs=out_specs, check_vma=False)

time: 754 us -> 363 us (0.48)
  Pallas kernels: 81.2 us -> 312 us
  blocking collectives: 220 us -> 0 us
  waiting for transfers between devices: 208 us -> 0.01 us
  matrix products: 157 us -> 5.91 us
  local copies, waits for them, and re-layouts: 31.1 us -> 14.1 us
  between operations: 15.9 us -> 0.81 us
  other arithmetic: 33.1 us -> 22.6 us
    pallas_call x0 -> x1, Pallas kernels: none -> 229 us  [main_call(): pl.pallas_call(functools.partial(main_kernel, wide), in_specs=[pl.BlockSp...]
    psum x1 -> x0, blocking collectives: 210 us -> none  [body(): lax.psum((d_w_qkv, d_b_qkv, d_w_dense, d_out_bias, d_ln_gain, d_ln_bias,...]
    psum x1 -> x0, waiting for transfers between devices: 158 us -> none  [body(): lax.psum((d_w_qkv, d_b_qkv, d_w_dense, d_out_bias, d_ln_gain, d_ln_bias,...]
    dot_general x11 -> x1, matrix products: 157 us -> 5.91 us  [dot_nt(): lax.dot_general(left, right, (((1,), (1,)), ((), ())), preferred_element_...]
    reduce_scatter x4 -> x0, waiting for transfers between devices: 36.3 us -> none  [the longest x2 36.3 us: body(): lax.psum_scatter(lax.optimization_barrier(partial_low).astype(jnp.float32...]
    unnamed x51 -> x22, local copies, waits for them, and re-layouts: 27.3 us -> 7.73 us
    all_gather x2 -> x0, waiting for transfers between devices: 13.3 us -> none  [the longest x1 13.3 us: body(): grad_all = lax.all_gather(cotangent, 'narrow', axis=0, tiled=True)]
    reduce_sum x4 -> x0, other arithmetic: 10.2 us -> none  [the longest x1 4.03 us: body(): d_b_qkv = jnp.sum(grad_proj.astype(jnp.float32), axis=0)]
  transfers between devices with their start and end apart: 7 -> 4, of which waited for: 3 -> 0; matrix products, arithmetic and copies ran while one was open for 25% -> 3% of each run, Pallas kernels for 8% -> 23%
where the time goes in v2:
time: 363 us
  Pallas kernels  312 us (86%)
  other arithmetic  22.6 us (6%)
  local copies, waits for them, and re-layouts  14.1 us (4%)
  starting transfers between devices  6.59 us (2%)
  matrix products  5.91 us (2%)
    pallas_call x1, Pallas kernels, main_call(): pl.pallas_call(functools.partial(main_kernel, wide), in_specs=[pl.BlockSp...  229 us
    pallas_call x1, Pallas kernels, attend(): pl.pallas_call(attention_kernel, grid_spec=pltpu.PrefetchScalarGridSpec(n...  60.1 us
    pallas_call x1, Pallas kernels, project(): pl.pallas_call(qkv_kernel, grid=(w_qkv.shape[1] // cols,), in_specs=[whol...  23.1 us
    unnamed x22, local copies, waits for them, and re-layouts  7.73 us
  transfers between devices with their start and end apart: 4, of which 0 were waited for; matrix products, arithmetic and copies ran while one was open for 3% of the time, Pallas kernels for 23%

profile of v2, /device:TPU:0, one launch (start us, length us, event | category | flops | bytes accessed | tf_op | source)
XLA Modules:
  0.0 362.6 jit_solution(14953650398631342662)
XLA Ops:
  0.7 0.7 broadcast_in_dim.72
  1.4 2.9 copy.24
  4.2 0.0 copy-start.4
  4.2 0.0 copy-start.6
  4.3 0.0 copy-start.7
  4.3 0.0 copy-start.8
  4.3 0.0 copy-start.5
  4.3 1.8 fusion.1.own_w
  6.1 0.0 copy-start
  6.1 2.0 copy-done
  8.1 0.1 dynamic-slice_bitcast_fusion
  8.1 3.0 collective-permute-start
  11.2 0.0 copy-done.4
  11.2 0.6 convert_reduce_fusion
  11.8 0.0 copy-start.3
  11.8 0.1 slice.30
  11.9 0.5 and_select_fusion.first_ref
  12.4 0.0 copy-done.6
  12.4 0.6 broadcast_in_dim.76
  13.0 0.0 copy-done.7
  13.0 0.6 broadcast_in_dim.77
  13.6 0.0 copy-done.8
  13.6 0.6 broadcast_in_dim.79
  14.2 0.0 copy-done.5
  14.2 0.6 broadcast_in_dim.78
  14.8 3.2 fusion.2
  18.0 5.9 %convolution_convert_fusion.g_ref = bf16[1024,1024]{1,0:T(8,128)(2,1)} fusion(bf16[1024,1024]{1,0:T(8,128)(2,1)} %cot.1, bf16[1024,1024]{1,0:T(8,128)(2,1)} %w_dense.1), kind=kOutput, calls=%fused_computation.7 | convolution fusion | flops 2148532224 | bytes 6291456 | tf_op jit(solution)/shard_map/dot_general | solution.py:51
  23.9 0.0 copy-done.3
  23.9 23.1 %shard_map.206 = (bf16[1024,3072]{1,0:T(8,128)(2,1)}, bf16[1024,1024]{1,0:T(8,128)(2,1)}, bf16[1024,1024]{1,0:T(8,128)(2,1)}) custom-call(bf16[1024,1024]{1,0:T(8,128)(2,1)} %tokens.1, f32[1,1024]{1,0:T(1,128)} %bitcast.32, f32[1,1024]{1,0:T(1,128)} %bitcast.35, bf16[1024,3072]{1,0:T(8,128)(2,1)} %w_qkv.1, f32[1,3072]{1,0:T(1,128)} %bitcast.31, ...), custom_call_target="tpu_custom_call" | custom-call | flops 6442450944 | bytes 16777216 | tf_op jit(solution)/shard_map/pallas_call | solution.py:104
  47.0 0.0 collective-permute-done
  47.0 2.6 collective-permute-start.3
  49.5 0.4 collective-permute-start.2
  50.0 0.5 collective-permute-start.1
  50.5 60.1 %shard_map.207 = (bf16[1024,1024]{1,0:T(8,128)(2,1)}, bf16[3,1024,1024]{2,1,0:T(8,128)(2,1)}) custom-call(s32[4]{0:T(128)} %and_select_fusion.first_ref, s32[1,1024]{1,0:T(1,128)} %bitcast.29, bf16[1024,3072]{1,0:T(8,128)(2,1)} %get-tuple-element.32.q_ref.k_ref.v_ref, bf16[1024,3072]{1,0:T(8,128)(2,1)} %get-tuple-element.32.q_ref.k_ref.v_ref, ...), custom_call_target="tpu_custom_call" | custom-call | flops 17179869184 | bytes 16777216 | tf_op jit(solution)/shard_map/pallas_call | solution.py:233
  110.6 0.0 collective-permute-done.3
  110.6 0.0 collective-permute-done.2
  110.6 0.0 collective-permute-done.1
  110.6 3.4 pad_maximum_fusion.y_w
  114.0 229.3 %shard_map.208 = (bf16[1024,1024]{1,0:T(8,128)(2,1)}, bf16[1024,1024]{1,0:T(8,128)(2,1)}, bf16[1024,1792]{1,0:T(8,128)(2,1)}, bf16[1280,1024]{1,0:T(8,128)(2,1)}...) custom-call(bf16[1024,1024]{1,0:T(8,128)(2,1)} %tokens.1, ...), custom_call_target="tpu_custom_call" | custom-call | flops 75161927680 | bytes 83886080 | tf_op jit(solution)/shard_map/pallas_call | solution.py:867
  343.3 1.4 fusion.11
  344.7 0.7 slice.34
  345.4 0.7 slice_bitcast_fusion
  346.1 2.1 slice_convert_fusion.3
  348.3 0.0 copy-start.1
  348.3 4.2 %slice_convert_fusion = f32[1024,1024]{1,0:T(8,128)} fusion(bf16[1280,1024]{1,0:T(8,128)(2,1)} %get-tuple-element.44), kind=kLoop, calls=%fused_computation.5 | loop fusion | flops 1048576 | bytes 6291456 | tf_op jit(solution)/shard_map/convert_element_type | solution.py:1008
  352.5 0.0 copy-done.1
  352.5 1.9 slice_convert_fusion.2
  354.4 2.6 slice_convert_fusion.1
  357.0 0.0 copy-start.2
  357.0 0.6 copy.25
  357.6 0.6 reshape.151
  358.2 3.1 copy.28
  361.2 0.0 copy-done.2
  361.3 1.3 copy.29
  (5 shorter events, 0.0 us)
Async XLA Ops:
  4.2 7.0 %copy-start.4 = (s32[1,1024]{1,0:T(1,128)S(1)}, s32[1,1024]{1,0:T(1,128)}, u32[]{:S(2)}) copy-start(s32[1,1024]{1,0:T(1,128)} %param.13) | copy-start | bytes 12292
  4.2 8.1 %copy-start.6 = (bf16[1024]{0:T(1024)(128)(2,1)S(1)}, bf16[1024]{0:T(1024)(128)(2,1)}, u32[]{:S(2)}) copy-start(bf16[1024]{0:T(1024)(128)(2,1)} %param.14) | copy-start | bytes 6148
  4.3 8.7 %copy-start.7 = (bf16[1024]{0:T(1024)(128)(2,1)S(1)}, bf16[1024]{0:T(1024)(128)(2,1)}, u32[]{:S(2)}) copy-start(bf16[1024]{0:T(1024)(128)(2,1)} %param.15) | copy-start | bytes 6148
  4.3 9.3 %copy-start.8 = (bf16[1024]{0:T(1024)(128)(2,1)S(1)}, bf16[1024]{0:T(1024)(128)(2,1)}, u32[]{:S(2)}) copy-start(bf16[1024]{0:T(1024)(128)(2,1)} %param.22) | copy-start | bytes 6148
  4.3 9.9 %copy-start.5 = (bf16[3072]{0:T(1024)(128)(2,1)S(1)}, bf16[3072]{0:T(1024)(128)(2,1)}, u32[]{:S(2)}) copy-start(bf16[3072]{0:T(1024)(128)(2,1)} %param.17) | copy-start | bytes 18436
  6.1 2.0 copy-start
  8.1 38.8 %collective-permute-start = (bf16[528,1024]{1,0:T(8,128)(2,1)S(1)}, bf16[528,1024]{1,0:T(8,128)(2,1)S(1)}, u32[]{:S(2)}, u32[]{:S(2)}) collective-permute-start(bf16[528,1024]{1,0:T(8,128)(2,1)S(1)} %dynamic-slice_bitcast_fusion), channel_id=1, source_target_pairs={{0,2},{1,3},{2,0},{3,1},{4,6},{5,7},{6,4},{7,5},{8,10},{9,11},{10,... | collective-permute-start | bytes 3244040 | tf_op jit(solution)/shard_map/ppermute | solution.py:933
  11.8 12.1 %copy-start.3 = (s32[1024]{0:T(1024)}, s32[1024]{0:T(1024)S(1)}, u32[]{:S(2)}) copy-start(s32[1024]{0:T(1024)S(1)} %convert_reduce_fusion) | copy-start | bytes 12292
  47.0 63.6 %collective-permute-start.3 = (bf16[528,1024]{1,0:T(8,128)(2,1)S(1)}, bf16[528,1024]{1,0:T(8,128)(2,1)S(1)}, u32[]{:S(2)}, u32[]{:S(2)}) collective-permute-start(bf16[528,1024]{1,0:T(8,128)(2,1)S(1)} %collective-permute-done), channel_id=1, source_target_pairs={{0,12},{4,8},{8,4},{12,0},{16,28},{20,24},{24,20},{28,16},{1,13},{... | collective-permute-start | bytes 3244040 | tf_op jit(solution)/shard_map/ppermute | solution.py:933
  49.5 61.1 %collective-permute-start.2 = (bf16[528,1024]{1,0:T(8,128)(2,1)S(1)}, bf16[528,1024]{1,0:T(8,128)(2,1)S(1)}, u32[]{:S(2)}, u32[]{:S(2)}) collective-permute-start(bf16[528,1024]{1,0:T(8,128)(2,1)S(1)} %collective-permute-done), channel_id=1, source_target_pairs={{0,8},{4,12},{8,0},{12,4},{16,24},{20,28},{24,16},{28,20},{1,9},{5... | collective-permute-start | bytes 3244040 | tf_op jit(solution)/shard_map/ppermute | solution.py:933
  50.0 60.6 %collective-permute-start.1 = (bf16[528,1024]{1,0:T(8,128)(2,1)S(1)}, bf16[528,1024]{1,0:T(8,128)(2,1)}, u32[]{:S(2)}, u32[]{:S(2)}) collective-permute-start(bf16[528,1024]{1,0:T(8,128)(2,1)S(1)} %collective-permute-done), channel_id=1, source_target_pairs={{0,4},{4,0},{8,12},{12,8},{16,20},{20,16},{24,28},{28,24},{1,5},{5... | collective-permute-start | bytes 3244040 | tf_op jit(solution)/shard_map/ppermute | solution.py:933
  348.3 4.2 %copy-start.1 = (bf16[1024,1792]{1,0:T(8,128)(2,1)S(1)}, bf16[1024,1792]{1,0:T(8,128)(2,1)}, u32[]{:S(2)}) copy-start(bf16[1024,1792]{1,0:T(8,128)(2,1)} %get-tuple-element.43) | copy-start | bytes 11010052
  357.0 4.3 %copy-start.2 = (bf16[1024,1024]{1,0:T(8,128)(2,1)S(1)}, bf16[1024,1024]{1,0:T(8,128)(2,1)}, u32[]{:S(2)}) copy-start(bf16[1024,1024]{1,0:T(8,128)(2,1)} %get-tuple-element.65) | copy-start | bytes 6291460

commit v3 on v2

v3 whole, which is shorter than its diff:
```python
import functools
import math

import jax
import jax.numpy as jnp
from jax import lax
from jax.experimental import pallas as pl
from jax.experimental.pallas import tpu as pltpu
from jax.sharding import PartitionSpec as P

D = 1024
HEADS = 16
HEAD = 64
ROT = 16
TILE = 256
PAIR = 2 * HEAD
MAX_DOC = 512
MESH = pl.DeviceIdType.MESH

MLP, DENSE, QKV, BLOCKS, GAP = 8, 8, 9, 12, 8
F_RING, Y_RING, S_RING = 8, 6, 2
LAGS = (4, 5, 6, 7, 8, 9)
CORE, YAXIS, XHALF, NEAR, BACK, WIDE_A, WIDE_B, KINDS = range(8)
ORDER = (3, 1, 2, 0)


def doc_starts(segments):
    return jnp.sum((segments[:, :, None] > segments[:, None, :]).astype(jnp.int32), axis=2)


def rope_tables(position):
    half_rot = ROT // 2
    lane = jnp.arange(PAIR, dtype=jnp.int32) % HEAD
    inv_freq = 1.0 / 10000.0 ** ((lane % half_rot).astype(jnp.float32) * 2.0 / ROT)
    angles = position.astype(jnp.float32)[:, None] * inv_freq[None, :]
    rotated = (lane < ROT)[None, :]
    sin = jnp.where((lane < half_rot)[None, :], -jnp.sin(angles), jnp.sin(angles))
    return jnp.where(rotated, jnp.cos(angles), 1.0), jnp.where(rotated, sin, 0.0)


def turn(t, same, partner):
    half_rot = ROT // 2
    lane = lax.broadcasted_iota(jnp.int32, t.shape, 1) % HEAD
    other = jnp.where(
        lane < half_rot,
        pltpu.roll(t, PAIR - half_rot, axis=1),
        pltpu.roll(t, half_rot, axis=1),
    )
    return t * same + other * partner


def dot_nt(left, right):
    return lax.dot_general(
        left, right, (((1,), (1,)), ((), ())), preferred_element_type=jnp.float32
    )


def dot_nn(left, right):
    return lax.dot_general(
        left, right, (((1,), (0,)), ((), ())), preferred_element_type=jnp.float32
    )


def xor2(value, other):
    return (value + other) % 2 + 2 * ((value // 2 + other // 2) % 2)


def gelu_parts(x):
    cdf = 0.5 * (1.0 + lax.erf(x * math.sqrt(0.5)))
    density = jnp.exp(-0.5 * x * x) * (1.0 / math.sqrt(2.0 * math.pi))
    return x * cdf, cdf + x * density


def widen(value):
    return value.astype(jnp.float32)


def low(value):
    return value.astype(jnp.bfloat16)


def block_of(v):
    late = MLP + GAP
    if isinstance(v, int):
        return (v if v < MLP else v - GAP), 0 <= v < MLP or late <= v < BLOCKS + GAP
    return (
        jnp.where(v < MLP, v, v - GAP),
        ((v >= 0) & (v < MLP)) | ((v >= late) & (v < BLOCKS + GAP)),
    )


def main_kernel(
    wide,
    tokens,
    cot,
    w_qkv,
    w_dense,
    w_up,
    w_down,
    same_in,
    partner_in,
    bias_in,
    start_ref,
    gain,
    ln_bias,
    b_qkv,
    out_bias,
    mixed_out,
    dtok_out,
    straight_out,
    turned_out,
    small_out,
    qkvg,
    att,
    gp,
    core_up,
    core_down,
    y_up,
    y_down,
    diag_up,
    diag_down,
    nrm,
    nrm_t,
    ct,
    ct_t,
    hid,
    gpre,
    pool,
    mixed_acc,
    gn_acc,
    slope,
    s_ring,
    a_ring,
    f_ring,
    r_ring,
    ry,
    rx,
    rz,
    rfar,
    gz,
    gx,
    tbuf,
    bias,
    sv,
    sv_sum,
    sv_recv,
    send,
    recv,
    far_send,
    far_recv,
    sv_send,
    sv_rsem,
    gy_send,
    gy_recv,
    gw_send,
    gw_recv,
    gc_send,
    gc_recv,
    gb_send,
    gb_recv,
    load,
    load_w,
    load_a,
    out_sem,
    free,
    y_free,
):
    rows = nrm.shape[0]
    R_RING, A_RING = r_ring.shape[0], a_ring.shape[0]
    n, w = lax.axis_index("narrow"), lax.axis_index("wide")
    near = w % 4
    xbit, zbit = w % 2, (w // 2) % 2
    bits = [b for b in range(2, 20) if (1 << b) < wide]
    mate = {"narrow": n + 1 - 2 * (n % 2)}
    ymate = {"narrow": n + 2 - 4 * (n // 2)}

    def across(bit):
        return {"wide": w + (1 << bit) - (2 << bit) * ((w // (1 << bit)) % 2)}

    def near_mate(k):
        return {"wide": w - near + xor2(near, k)}

    def spot(r):
        return xor2(n, r)

    def tiles(start, size=TILE):
        return pl.ds(pl.multiple_of(start, TILE), size)

    def remote_to(src, dst, send_sem, recv_sem, dev):
        return pltpu.make_async_remote_copy(
            src_ref=src,
            dst_ref=dst,
            send_sem=send_sem,
            recv_sem=recv_sem,
            device_id=dev,
            device_id_type=MESH,
        )

    def copy_in(src, dst, i):
        return pltpu.make_async_copy(src, dst, load.at[i])

    firsts = [
        copy_in(tokens, hid, 0),
        copy_in(same_in, slope.at[:, 2 * PAIR : 3 * PAIR], 1),
        copy_in(partner_in, slope.at[:, 3 * PAIR : 4 * PAIR], 2),
        copy_in(w_qkv.at[:, 0:rows], pool.at[1], 3),
        copy_in(w_qkv.at[:, rows : 2 * rows], pool.at[2], 4),
        copy_in(w_qkv.at[:, 2 * rows : 3 * rows], pool.at[3], 5),
        copy_in(w_dense, pool.at[0], 6),
        copy_in(cot, ct, 7),
    ]
    own_bias = copy_in(bias_in, bias.at[0], 8)
    for c in firsts:
        c.start()
    own_bias.start()

    partners = [mate, ymate, near_mate(3)] + [across(b) for b in [0, 1] + bits]
    barrier = pltpu.get_barrier_semaphore()
    for p in partners:
        pl.semaphore_signal(barrier, inc=1, device_id=p, device_id_type=MESH)
    pl.semaphore_wait(barrier, len(partners))

    def gather_y(k, a):
        if k == 0:
            src, dst = w_up.at[tiles(near * TILE), tiles(a * TILE)], y_up.at[a, tiles(near * TILE)]
        else:
            src = w_down.at[tiles(a * TILE), tiles(near * TILE)]
            dst = y_down.at[a, :, tiles(near * TILE)]
        return remote_to(src, dst, gy_send.at[k, a], gy_recv.at[k, a], ymate)

    def gather_near(k, a, to):
        ref = y_up.at[a, tiles(near * TILE)] if k == 0 else y_down.at[a, :, tiles(near * TILE)]
        return remote_to(
            ref, ref, gw_send.at[k, a, to - 1], gw_recv.at[k, a, to - 1], near_mate(to)
        )

    def gather_core(k, a):
        src = (
            w_up.at[:, tiles(a * TILE)],
            w_down.at[tiles(a * TILE)],
            y_up.at[a],
            y_down.at[a],
        )[k]
        dst = (core_up, core_down, diag_up, diag_down)[k].at[a]
        return remote_to(src, dst, gc_send.at[k, a], gc_recv.at[k, a], mate)

    def gather_bias(i):
        src = (0, 0, 2)[i]
        dst = (1, 2, 3)[i]
        dev = (mate, ymate, mate)[i]
        return remote_to(bias.at[src], bias.at[dst], gb_send.at[i], gb_recv.at[i], dev)

    def arrived_y(a):
        for k in range(2):
            gather_y(k, a).wait_recv()
            for to in (1, 2, 3):
                gather_near(k, a, to).start()

    def arrived_near(a):
        for k in range(2):
            for to in (1, 2, 3):
                gather_near(k, a, to).wait_recv()
            gather_core(2 + k, a).start()

    def weights(a):
        slot = a % 2
        copies = []
        for p, r in enumerate(ORDER):
            src = (
                (w_up.at[:, tiles(a * TILE)], w_down.at[tiles(a * TILE)]),
                (core_up.at[a], core_down.at[a]),
                (y_up.at[a], y_down.at[a]),
                (diag_up.at[a], diag_down.at[a]),
            )[r]
            cols = slice(p * TILE, (p + 1) * TILE)
            copies.append(
                pltpu.make_async_copy(src[0], pool.at[2 * slot, :, cols], load_w.at[slot, p])
            )
            copies.append(
                pltpu.make_async_copy(src[1], pool.at[2 * slot + 1, cols], load_w.at[slot, 4 + p])
            )
        return copies

    def weights_here(a):
        for k in range(4):
            gather_core(k, a).wait_recv()
        for c in weights(a):
            c.start()

    for a in range(4):
        for k in range(2):
            gather_y(k, a).start()
            gather_core(k, a).start()
    own_bias.wait()
    gather_bias(0).start()
    gather_bias(1).start()

    sv[...] = jnp.zeros_like(sv)
    firsts[0].wait()

    def norm(m, c):
        at = tiles(m * TILE)
        x = widen(hid[at, :])
        mean = jnp.mean(x, axis=-1, keepdims=True)
        centered = x - mean
        variance = jnp.mean(centered * centered, axis=-1, keepdims=True)
        normed = centered * lax.rsqrt(variance + 1e-05) * gain[...] + ln_bias[...]
        nrm[at, :] = low(normed)
        nrm_t[:, at] = low(normed.T)
        return c

    lax.fori_loop(0, rows // TILE, norm, 0)
    half = rows // 2

    def store_out(i, buf):
        return pltpu.make_async_copy(buf, qkvg.at[i], load.at[i])

    buffers = (hid, gpre, hid, gpre)
    for i in range(4):
        buf = buffers[i]
        if i == 0:
            firsts[1].wait()
            firsts[2].wait()
        if i >= 2:
            store_out(i - 2, buf).wait()
        if i < 3:
            firsts[3 + i].wait()
        else:
            firsts[6].wait()
            firsts[7].wait()

        def project(m, c, i=i, buf=buf):
            at = pl.ds(pl.multiple_of(m * half, half), half)
            if i == 3:
                buf[at, :] = low(dot_nt(ct[at, :], pool[0]))
                return c
            got = dot_nn(nrm[at, :], pool[1 + i]) + b_qkv[0:1, i * rows : (i + 1) * rows]
            if i == 2:
                buf[at, :] = low(got)
                return c
            same, partner = slope[at, 2 * PAIR : 3 * PAIR], slope[at, 3 * PAIR : 4 * PAIR]
            for k in range(0, rows, PAIR):
                t = turn(got[:, k : k + PAIR], same, partner)
                if i == 0:
                    t = t * (1.0 / math.sqrt(HEAD))
                buf[at, k : k + PAIR] = low(t)
            return c

        lax.fori_loop(0, 2, project, 0)
        store_out(i, buf).start()
        if i > 0:
            arrived_y(i - 1)
    gather_bias(1).wait_recv()
    gather_bias(2).start()

    def turn_cot(m, c):
        at = tiles(m * TILE)
        ct_t[:, at] = low(widen(ct[at, :]).T)
        return c

    lax.fori_loop(0, rows // TILE, turn_cot, 0)
    mixed_acc[...] = jnp.zeros_like(mixed_acc)
    gn_acc[...] = jnp.zeros_like(gn_acc)
    arrived_near(0)
    arrived_y(3)
    store_out(2, hid).wait()
    store_out(3, gpre).wait()
    gather_bias(0).wait_recv()
    gather_bias(2).wait_recv()

    quarter = rows // 4
    own_half, other_half = half * xbit, half * (1 - xbit)
    own_q = own_half + quarter * zbit
    other_q = own_half + quarter * (1 - zbit)

    def seg(start, size):
        return pl.ds(pl.multiple_of(start, quarter), size)

    def remote(src, dst, kind, b, dev):
        return remote_to(src, dst, send.at[kind, b], recv.at[kind, b], dev)

    def core_copy(b):
        return remote(s_ring.at[b % S_RING], r_ring.at[b % R_RING], CORE, b, mate)

    def y_copy(b):
        return remote(a_ring.at[b % A_RING], ry.at[b % Y_RING], YAXIS, b, ymate)

    def x_copy(b):
        return remote(f_ring.at[b % F_RING, seg(other_half, half)], rx.at[b], XHALF, b, across(0))

    def z_copy(b):
        return remote(f_ring.at[b % F_RING, seg(other_q, quarter)], rz.at[b], NEAR, b, across(1))

    def far_copy(i, b):
        return remote_to(
            f_ring.at[b % F_RING, seg(own_q, quarter)],
            rfar.at[i, b],
            far_send.at[i, b],
            far_recv.at[i, b],
            across(bits[i]),
        )

    def back_z(b):
        return remote(f_ring.at[b % F_RING, seg(own_q, quarter)], gz.at[b], BACK, b, across(1))

    def back_xa(b):
        return remote(
            f_ring.at[b % F_RING, seg(own_q, quarter)], gx.at[b, 0], WIDE_A, b, across(0)
        )

    def back_xb(b):
        return remote(gz.at[b], gx.at[b, 1], WIDE_B, b, across(0))

    def is_turned(b):
        return (b % 2 == 0) & (b <= DENSE)

    def piece(i, b):
        src = (
            f_ring.at[b % F_RING, seg(own_q, quarter)],
            gz.at[b],
            gx.at[b, 0],
            gx.at[b, 1],
        )[i]
        at = own_half if i < 2 else other_half
        return src, at + quarter * (zbit if i % 2 == 0 else 1 - zbit)

    def straight_copy(i, b):
        src, at = piece(i, b)
        column = jnp.where(b < MLP, b // 2, b - QKV + MLP // 2)
        return pltpu.make_async_copy(
            src, straight_out.at[seg(at, quarter), tiles(column * TILE)], out_sem.at[i, b]
        )

    def turned_copy(i, b):
        src, at = piece(i, b)
        return pltpu.make_async_copy(
            tbuf.at[(b // 2) % 2, i],
            turned_out.at[tiles((b // 2) * TILE), seg(at, quarter)],
            out_sem.at[i, b],
        )

    def put(i, b):
        @pl.when(is_turned(b))
        def _():
            src, at = piece(i, b)
            tbuf[(b // 2) % 2, i] = low(widen(src[...]).T)
            turned_copy(i, b).start()

        @pl.when(jnp.logical_not(is_turned(b)))
        def _():
            straight_copy(i, b).start()

    def add_into(b, start, size, other):
        at = seg(start, size)
        slot = b % F_RING
        f_ring[slot, at] = low(widen(f_ring[slot, at]) + widen(other[...]))

    def stage_y(b):
        y_copy(b).wait_recv()
        add_into(b, other_half, half, ry.at[b % Y_RING, seg(other_half, half)])
        x_copy(b).start()
        add_into(b, own_half, half, ry.at[b % Y_RING, seg(own_half, half)])

        @pl.when(b + Y_RING < BLOCKS)
        def _():
            pl.semaphore_signal(y_free, inc=1, device_id=ymate, device_id_type=MESH)

    def stage_x(b):
        x_copy(b).wait_recv()
        add_into(b, other_q, quarter, rx.at[b, seg(quarter * (1 - zbit), quarter)])
        z_copy(b).start()
        add_into(b, own_q, quarter, rx.at[b, seg(quarter * zbit, quarter)])

    def stage_near(b):
        z_copy(b).wait_recv()
        add_into(b, own_q, quarter, rz.at[b])
        far_copy(0, b).start()

    def stage_far(b):
        for i in range(len(bits)):
            far_copy(i, b).wait()
            add_into(b, own_q, quarter, rfar.at[i, b])
            if i + 1 < len(bits):
                far_copy(i + 1, b).start()
        back_z(b).start()
        back_xa(b).start()
        put(0, b)
        x_copy(b).wait_send()
        z_copy(b).wait_send()

    def stage_back(b):
        back_z(b).wait_recv()
        back_xb(b).start()
        put(1, b)

    def stage_out(b):
        back_xa(b).wait_recv()
        put(2, b)
        back_xb(b).wait_recv()
        put(3, b)
        back_z(b).wait_send()
        back_xa(b).wait_send()
        back_xb(b).wait_send()
        for i in range(4):
            straight_copy(i, b).wait()

    stages = (stage_y, stage_x, stage_near, stage_far, stage_back, stage_out)

    def progress(v):
        for lag, stage in reversed(list(zip(LAGS, stages))):
            b, there = block_of(v - lag)

            @pl.when(there)
            def _(stage=stage, b=b):
                stage(b)

    def parts_away(b, left, right):
        @pl.when(b >= S_RING)
        def _():
            core_copy(b - S_RING).wait_send()

        s_ring[b % S_RING] = low(dot_nn(left[...], right[...]))

        @pl.when(b >= R_RING)
        def _():
            pl.semaphore_wait(free, 1)

        core_copy(b).start()

    def parts_here(b, left, right):
        @pl.when(b >= A_RING)
        def _():
            y_copy(b - A_RING).wait_send()

        core_copy(b).wait_recv()
        got = dot_nn(left[...], right[...]) + widen(r_ring[b % R_RING])
        a_ring[b % A_RING] = low(got[:, :TILE])

        @pl.when(b >= Y_RING)
        def _():
            pl.semaphore_wait(y_free, 1)

        y_copy(b).start()
        f_ring[b % F_RING] = low(got[:, TILE:])

        @pl.when(b + R_RING < BLOCKS)
        def _():
            pl.semaphore_signal(free, inc=1, device_id=mate, device_id_type=MESH)

    def accumulate(target, left, right, dot):
        def chunk(m, c):
            at = pl.ds(pl.multiple_of(m * half, half), half)
            target[at, :] += dot(left[at, :], right[...])
            return c

        lax.fori_loop(0, 2, chunk, 0)

    def in_pair(i, s):
        cols = tiles_pair(i)
        return [
            pltpu.make_async_copy(
                qkvg.at[c, :, cols], pool.at[s, :, c * PAIR : (c + 1) * PAIR], load_a.at[s, c]
            )
            for c in range(4)
        ]

    def tiles_pair(i):
        return pl.ds(pl.multiple_of(i * PAIR, PAIR), PAIR)

    weights_here(0)

    def mlp_block(cb, carry):
        slot = cb % 2
        for c in weights(cb):
            c.wait()

        @pl.when(cb == 3)
        def _():
            for c in in_pair(0, 0):
                c.start()

        for side in range(2):
            cols = slice(side * 2 * TILE, (side + 1) * 2 * TILE)
            up, down = pool.at[2 * slot, :, cols], pool.at[2 * slot + 1, cols]
            at = tiles(cb * TILE)
            bias_row = jnp.concatenate(
                [bias[ORDER[2 * side], 0:1, at], bias[ORDER[2 * side + 1], 0:1, at]], axis=1
            )

            def act(m, c):
                at = pl.ds(pl.multiple_of(m * half, half), half)
                value, grad = gelu_parts(dot_nn(nrm[at, :], up[...]) + bias_row)
                hid[at, cols] = low(value)
                slope[at, :] = grad
                return c

            lax.fori_loop(0, 2, act, 0)
            parts = (parts_away, parts_here)[side]
            parts(2 * cb, ct_t, hid.at[:, cols])
            if side == 0:

                @pl.when(cb < 3)
                def _():
                    arrived_near(cb + 1)

            else:
                progress(2 * cb)

            def back(m, total):
                at = pl.ds(pl.multiple_of(m * half, half), half)
                got = low(dot_nt(ct[at, :], down[...]) * slope[at, :])
                gpre[at, cols] = got
                return total + jnp.sum(widen(got), axis=0, keepdims=True)

            total = lax.fori_loop(0, 2, back, jnp.zeros((1, 2 * TILE), jnp.float32))
            for k in range(2):
                sv[ORDER[2 * side + k], pl.ds(6 + cb, 1), :] = total[:, k * TILE : (k + 1) * TILE]
            parts(2 * cb + 1, nrm_t, gpre.at[:, cols])

        @pl.when(cb < 3)
        def _():
            weights_here(cb + 1)

        accumulate(mixed_acc, hid, pool.at[2 * slot + 1], dot_nn)
        accumulate(gn_acc, gpre, pool.at[2 * slot], dot_nt)
        progress(2 * cb + 1)
        return carry

    lax.fori_loop(0, 4, mlp_block, 0)

    tables = [
        copy_in(same_in, slope.at[:, 2 * PAIR : 3 * PAIR], 0),
        copy_in(partner_in, slope.at[:, 3 * PAIR : 4 * PAIR], 1),
    ]
    for c in tables:
        c.start()

    def ordered(j, ref, i, by_rows):
        copies = []
        for p, r in enumerate(ORDER):
            cols = slice(p * TILE, (p + 1) * TILE)
            if by_rows:
                src, dst = w_dense.at[tiles(spot(r) * TILE)], ref.at[cols]
            else:
                src, dst = w_qkv.at[:, tiles((3 * spot(r) + j) * TILE)], ref.at[:, cols]
            copies.append(pltpu.make_async_copy(src, dst, load_w.at[i, p]))
        return copies

    later = [ordered(0, hid, 0, False), ordered(1, gpre, 1, False)]
    for group in later:
        for c in group:
            c.start()
    for c in tables:
        c.wait()

    def out_pair(i, s):
        cols = tiles_pair(i)
        dsts = [att.at[:, cols]] + [gp.at[c, :, cols] for c in range(3)]
        return [
            pltpu.make_async_copy(
                pool.at[s, :, (4 + c) * PAIR : (5 + c) * PAIR], dsts[c], load_a.at[s, 4 + c]
            )
            for c in range(4)
        ]

    def attention(i, carry):
        s = i % 2
        for c in in_pair(i, s):
            c.wait()

        @pl.when(i + 1 < GAP)
        def _():
            for c in in_pair(i + 1, 1 - s):
                c.start()

        @pl.when(i >= 2)
        def _():
            for c in out_pair(i - 2, s):
                c.wait()

        def view(c):
            return pool.at[s, :, c * PAIR : (c + 1) * PAIR]

        q_ref, k_ref, v_ref, g_ref, att_ref, dq_ref, dk_ref, dv_ref = map(view, range(8))
        kt_ref, vt_ref = pool.at[2, 0:PAIR], pool.at[2, PAIR : 2 * PAIR]
        dk_acc, dv_acc = slope.at[:, 0:PAIR], slope.at[:, PAIR : 2 * PAIR]
        same_ref, partner_ref = (
            slope.at[:, 2 * PAIR : 3 * PAIR],
            slope.at[:, 3 * PAIR : 4 * PAIR],
        )
        lane = lax.broadcasted_iota(jnp.int32, (1, PAIR), 1)
        dk_acc[...] = jnp.zeros((rows, PAIR), jnp.float32)
        dv_acc[...] = jnp.zeros((rows, PAIR), jnp.float32)
        kt_ref[...] = low(widen(k_ref[...]).T)
        vt_ref[...] = low(widen(v_ref[...]).T)
        for block in range(rows // TILE):
            first = max(0, block - MAX_DOC // TILE)
            here = slice(block * TILE, (block + 1) * TILE)
            q_pair, g_pair = q_ref[here, :], g_ref[here, :]
            start = start_ref[:, here]
            query_index = block * TILE + lax.broadcasted_iota(jnp.int32, (1, TILE), 1)
            keys = [slice(j * TILE, (j + 1) * TILE) for j in range(first, block + 1)]
            visible = []
            for k in keys:
                index = k.start + lax.broadcasted_iota(jnp.int32, (TILE, TILE), 0)
                seen = index >= start
                visible.append(seen & (index <= query_index) if k.start == here.start else seen)
            out_t, dq_t = [], []
            for head in range(2):
                mine = (lane >= head * HEAD) & (lane < (head + 1) * HEAD)
                q = jnp.where(mine, q_pair, jnp.zeros_like(q_pair))
                g = jnp.where(mine, g_pair, jnp.zeros_like(g_pair))
                span = slice(head * HEAD, (head + 1) * HEAD)
                scores = [
                    jnp.where(see, dot_nt(k_ref[k, :], q), -1e30) for k, see in zip(keys, visible)
                ]
                grad_prob = [dot_nt(v_ref[k, :], g) for k in keys]
                top = functools.reduce(
                    jnp.maximum, [jnp.max(t, axis=0, keepdims=True) for t in scores]
                )
                exps = [jnp.exp(t - top) for t in scores]
                inverse = 1.0 / sum(jnp.sum(e, axis=0, keepdims=True) for e in exps)
                probs = [e * inverse for e in exps]
                row_dot = sum(
                    jnp.sum(p * d, axis=0, keepdims=True) for p, d in zip(probs, grad_prob)
                )
                out_head = jnp.zeros((HEAD, TILE), jnp.float32)
                dq_head = jnp.zeros((HEAD, TILE), jnp.float32)
                for k, p, d in zip(keys, probs, grad_prob):
                    p_low = low(p)
                    grad_score = low(p * (d - row_dot))
                    out_head += dot_nn(vt_ref[span, k], p_low)
                    dq_head += dot_nn(kt_ref[span, k], grad_score)
                    dv_acc[k, :] += dot_nn(p_low, g)
                    dk_acc[k, :] += dot_nn(grad_score, q)
                out_t.append(out_head)
                dq_t.append(dq_head)
            att_ref[here, :] = low(jnp.concatenate(out_t, axis=0).T)
            dq = jnp.concatenate(dq_t, axis=0).T * (1.0 / math.sqrt(HEAD))
            dq_ref[here, :] = low(turn(dq, same_ref[here, :], -partner_ref[here, :]))
        dk_ref[...] = low(turn(dk_acc[...], same_ref[...], -partner_ref[...]))
        dv_ref[...] = low(dv_acc[...])
        for c in out_pair(i, s):
            c.start()
        progress(MLP + i)
        return carry

    lax.fori_loop(0, GAP, attention, 0)
    for i in (GAP - 2, GAP - 1):
        for c in out_pair(i, i % 2):
            c.wait()

    def att_tiles():
        return [
            pltpu.make_async_copy(
                att.at[:, tiles(spot(r) * TILE)],
                pool.at[0, :, p * TILE : (p + 1) * TILE],
                load_w.at[2, p],
            )
            for p, r in enumerate(ORDER)
        ]

    def gp_tiles(j):
        copies = []
        for p, r in enumerate(ORDER):
            at = 3 * spot(r) + j
            copies.append(
                pltpu.make_async_copy(
                    gp.at[at // 4, :, tiles((at % 4) * TILE)],
                    pool.at[1 + j, :, p * TILE : (p + 1) * TILE],
                    load_w.at[3, 4 * j + p],
                )
            )
        return copies

    for c in att_tiles():
        c.start()
    for j in range(3):
        for c in gp_tiles(j):
            c.start()
    pair_a, pair_b = slice(0, 2 * TILE), slice(2 * TILE, 4 * TILE)
    for c in att_tiles():
        c.wait()
    parts_away(DENSE, ct_t, pool.at[0, :, pair_a])
    parts_here(DENSE, ct_t, pool.at[0, :, pair_b])
    progress(DENSE + GAP)

    def qkv_block(j, carry):
        for c in gp_tiles(j):
            c.wait()
        parts_away(QKV + j, nrm_t, pool.at[1 + j, :, pair_a])
        parts_here(QKV + j, nrm_t, pool.at[1 + j, :, pair_b])
        total = jnp.sum(widen(pool[1 + j]), axis=0, keepdims=True)
        for p, r in enumerate(ORDER):
            sv[r, pl.ds(3 + j, 1), :] = total[:, p * TILE : (p + 1) * TILE]
        progress(QKV + GAP + j)
        return carry

    lax.fori_loop(0, 3, qkv_block, 0)
    for group in later:
        for c in group:
            c.wait()
    accumulate(gn_acc, pool.at[1], hid, dot_nt)
    accumulate(gn_acc, pool.at[2], gpre, dot_nt)
    last = ordered(2, hid, 0, False) + ordered(0, gpre, 1, True)
    tok_load = copy_in(tokens, pool.at[1], 0)
    for c in last + [tok_load]:
        c.start()
    for c in last:
        c.wait()
    accumulate(gn_acc, pool.at[3], hid, dot_nt)
    accumulate(mixed_acc, pool.at[0], gpre, dot_nn)
    tok_load.wait()
    tick = BLOCKS + GAP
    progress(tick)

    def finish(m, sums):
        at = tiles(m * TILE)
        x = widen(pool[1, at, :])
        mean = jnp.mean(x, axis=-1, keepdims=True)
        centered = x - mean
        variance = jnp.mean(centered * centered, axis=-1, keepdims=True)
        inv_std = lax.rsqrt(variance + 1e-05)
        unit = centered * inv_std
        hid[at, :] = low(mixed_acc[at, :] + x + out_bias[...])
        gn = gn_acc[at, :]
        g = gn * gain[...]
        mean_grad = jnp.mean(g, axis=-1, keepdims=True)
        mean_proj = jnp.mean(g * unit, axis=-1, keepdims=True)
        c = widen(ct[at, :])
        gpre[at, :] = low(c + inv_std * (g - mean_grad - unit * mean_proj))
        return (
            sums[0] + jnp.sum(gn * unit, axis=0, keepdims=True),
            sums[1] + jnp.sum(gn, axis=0, keepdims=True),
            sums[2] + jnp.sum(c, axis=0, keepdims=True),
        )

    zero = jnp.zeros((1, rows), jnp.float32)
    sums = lax.fori_loop(0, rows // TILE, finish, (zero, zero, zero))
    final = [
        pltpu.make_async_copy(hid, mixed_out, load.at[1]),
        pltpu.make_async_copy(gpre, dtok_out, load.at[2]),
    ]
    for c in final:
        c.start()
    for i in range(3):
        sv_sum[i : i + 1, :] = sums[i]
    for r in range(4):
        sv[r, 0:3, :] = sv_sum[0:3, tiles(spot(r) * TILE)]

    def sv_copy(i, src, dev):
        return remote_to(src, sv_recv.at[i], sv_send.at[i], sv_rsem.at[i], dev)

    hops = [
        sv_copy(0, sv.at[1], mate),
        sv_copy(1, sv.at[3], mate),
        sv_copy(2, sv.at[2], ymate),
    ]
    hops += [sv_copy(3 + i, sv.at[0], across(b)) for i, b in enumerate([0, 1] + bits)]
    hops[0].start()
    hops[1].start()
    tick += 1
    progress(tick)
    hops[0].wait()
    hops[1].wait()
    sv[0] = sv[0] + sv_recv[0]
    sv[2] = sv[2] + sv_recv[1]
    hops[2].start()
    tick += 1
    progress(tick)
    hops[2].wait()
    sv[0] = sv[0] + sv_recv[2]
    for i in range(3, len(hops)):
        hops[i].start()
        tick += 1
        if tick < BLOCKS + GAP + LAGS[-1]:
            progress(tick)
        hops[i].wait()
        sv[0] = sv[0] + sv_recv[i]
    small_out[...] = sv[0]
    while tick + 1 < BLOCKS + GAP + LAGS[-1]:
        tick += 1
        progress(tick)

    for c in final:
        c.wait()
    for b in range(BLOCKS - S_RING, BLOCKS):
        core_copy(b).wait_send()
    for b in range(BLOCKS - A_RING, BLOCKS):
        y_copy(b).wait_send()
    for i in range(3):
        gather_bias(i).wait_send()
    for a in range(4):
        for k in range(2):
            gather_y(k, a).wait_send()
            for to in (1, 2, 3):
                gather_near(k, a, to).wait_send()
        for k in range(4):
            gather_core(k, a).wait_send()


def main_call(wide, hbm_args, vmem_args):
    tokens = hbm_args[0]
    rows, width = tokens.shape
    hops = max(wide.bit_length() - 1, 2)
    far = hops - 2
    bf, f32 = jnp.bfloat16, jnp.float32
    half, quarter = rows // 2, rows // 4
    vm = pltpu.VMEM
    dma = pltpu.SemaphoreType.DMA
    shape = jax.ShapeDtypeStruct
    any_space, vmem_space = (pl.BlockSpec(memory_space=s) for s in (pl.ANY, pltpu.VMEM))
    return pl.pallas_call(
        functools.partial(main_kernel, wide),
        in_specs=[any_space] * len(hbm_args) + [vmem_space] * len(vmem_args),
        out_specs=[any_space] * 4 + [vmem_space] + [any_space] * 9,
        out_shape=[
            shape((rows, width), bf),
            shape((rows, width), bf),
            shape((width, 7 * TILE), bf),
            shape((5 * TILE, width), bf),
            shape((16, TILE), f32),
            shape((4, rows, width), bf),
            shape((rows, width), bf),
            shape((3, rows, width), bf),
        ]
        + [shape((4, width, TILE), bf), shape((4, TILE, width), bf)] * 3,
        scratch_shapes=[
            vm((rows, width), bf),
            vm((width, rows), bf),
            vm((rows, width), bf),
            vm((width, rows), bf),
            vm((rows, width), bf),
            vm((rows, width), bf),
            vm((4, rows, width), bf),
            vm((rows, width), f32),
            vm((rows, width), f32),
            vm((rows, 2 * TILE), f32),
            vm((S_RING, width, 2 * TILE), bf),
            vm((4 if far < 2 else 2, width, TILE), bf),
            vm((F_RING, width, TILE), bf),
            vm((2, width, 2 * TILE), bf),
            vm((Y_RING, width, TILE), bf),
            vm((BLOCKS, half, TILE), bf),
            vm((BLOCKS, quarter, TILE), bf),
            vm((far, BLOCKS, quarter, TILE), bf),
            vm((BLOCKS, quarter, TILE), bf),
            vm((BLOCKS, 2, quarter, TILE), bf),
            vm((2, 4, TILE, TILE), bf),
            vm((4, 8, width), f32),
            vm((4, 16, TILE), f32),
            vm((8, width), f32),
            vm((3 + hops, 16, TILE), f32),
            dma((KINDS, BLOCKS)),
            dma((KINDS, BLOCKS)),
            dma((far, BLOCKS)),
            dma((far, BLOCKS)),
            dma((3 + hops,)),
            dma((3 + hops,)),
            dma((2, 4)),
            dma((2, 4)),
            dma((2, 4, 3)),
            dma((2, 4, 3)),
            dma((4, 4)),
            dma((4, 4)),
            dma((3,)),
            dma((3,)),
            dma((9,)),
            dma((4, 12)),
            dma((2, 8)),
            dma((4, BLOCKS)),
            pltpu.SemaphoreType.REGULAR,
            pltpu.SemaphoreType.REGULAR,
        ],
        compiler_params=pltpu.CompilerParams(
            collective_id=0, has_side_effects=True, vmem_limit_bytes=62 << 20
        ),
        cost_estimate=pl.CostEstimate(
            flops=90 * rows * width * width, bytes_accessed=100 << 20, transcendentals=0
        ),
    )(*hbm_args, *vmem_args)


def make_body(wide):
    def body(
        tokens,
        seg_ids,
        ln_gain,
        ln_bias,
        w_qkv,
        b_qkv,
        w_dense,
        w_up,
        b_up,
        w_down,
        out_bias,
        cotangent,
    ):
        seq_len = seg_ids.shape[1]
        starts = doc_starts(seg_ids)
        position = jnp.arange(seq_len, dtype=jnp.int32) - starts[0]
        same, partner = rope_tables(position)

        def row(vector):
            return vector.astype(jnp.float32)[None, :]

        bias_rows = jnp.broadcast_to(row(b_up), (8, b_up.shape[0]))
        mixed, d_tokens, straight, turned, small = main_call(
            wide,
            (tokens, cotangent, w_qkv, w_dense, w_up, w_down, same, partner, bias_rows),
            (starts, row(ln_gain), row(ln_bias), row(b_qkv), row(out_bias)),
        )[:5]
        split = MLP // 2 * TILE
        return (
            mixed,
            d_tokens,
            small[0],
            small[1],
            straight[:, split:].astype(jnp.float32),
            small[3:6].reshape(-1),
            turned[split:].astype(jnp.float32),
            straight[:, :split].astype(jnp.float32),
            small[6:10].reshape(-1),
            turned[:split].astype(jnp.float32),
            small[2],
        )

    return body


def solution(mesh):
    in_specs = (
        P(("wide", "narrow"), None),
        P(("wide", "narrow"), None),
        P(),
        P(),
        P(),
        P(),
        P(),
        P(None, "narrow"),
        P("narrow"),
        P("narrow", None),
        P(),
        P(("wide", "narrow"), None),
    )
    out_specs = (
        P(("wide", "narrow"), None),
        P(("wide", "narrow"), None),
        P("narrow"),
        P("narrow"),
        P(None, "narrow"),
        P("narrow"),
        P("narrow", None),
        P(None, "narrow"),
        P("narrow"),
        P("narrow", None),
        P("narrow"),
    )
    return jax.shard_map(
        make_body(mesh.shape["wide"]), mesh=mesh, in_specs=in_specs, out_specs=out_specs, check_vma=False)
```

time: 363 us -> 312 us (0.86)
  Pallas kernels: 312 us -> 281 us
  starting transfers between devices: 6.59 us -> 0 us
  matrix products: 5.91 us -> 0 us
  local copies, waits for them, and re-layouts: 14.1 us -> 8.98 us
    pallas_call x3 -> x1, Pallas kernels: 312 us -> 281 us  [main_call(): pl.pallas_call(functools.partial(main_kernel, wide), in_specs=[any_space]...]
    ppermute x4 -> x0, starting transfers between devices: 6.59 us -> none  [flip(): return lax.ppermute(value, axis, [(i, i ^ bit) for i in range(size)])]
    dot_general x1 -> x0, matrix products: 5.91 us -> none  [dot_nt(): lax.dot_general(left, right, (((1,), (1,)), ((), ())), preferred_element_...]
    unnamed x22 -> x12, local copies, waits for them, and re-layouts: 7.73 us -> 5 us
  transfers between devices with their start and end apart: 4 -> 0, of which waited for: 0 -> 0; matrix products, arithmetic and copies ran while one was open for 3% -> 0% of each run, Pallas kernels for 23% -> 0%
where the time goes in v3:
time: 312 us; the launch traced here: 311 us
  Pallas kernels  281 us (90%)
  other arithmetic  20.4 us (7%)
  local copies, waits for them, and re-layouts  8.98 us (3%)
    pallas_call x1, Pallas kernels, main_call(): pl.pallas_call(functools.partial(main_kernel, wide), in_specs=[any_space]...  281 us

profile of v3, /device:TPU:0, one launch (start us, length us, event | category | flops | bytes accessed | tf_op | source)
XLA Modules:
  0.0 311.0 jit_solution(17083964846586692957)
XLA Ops:
  0.7 1.3 convert_reduce_fusion
  2.0 0.0 copy-start.3
  2.0 1.3 broadcast_in_dim.73
  3.3 1.3 broadcast_in_dim.74
  4.6 1.3 broadcast_in_dim.76
  5.8 1.3 broadcast_in_dim.75
  7.1 1.3 broadcast_in_dim.64.bias_in
  8.4 3.1 fusion.1
  11.5 0.0 copy-done.3
  11.5 280.9 %shard_map.206 = (bf16[1024,1024]{1,0:T(8,128)(2,1)}, bf16[1024,1024]{1,0:T(8,128)(2,1)}, bf16[1024,1792]{1,0:T(8,128)(2,1)}, bf16[1280,1024]{1,0:T(8,128)(2,1)}...) custom-call(bf16[1024,1024]{1,0:T(8,128)(2,1)} %tokens.1, ...), custom_call_target="tpu_custom_call" | custom-call | flops 96636764160 | bytes 104857600 | tf_op jit(solution)/shard_map/pallas_call | solution.py:913
  292.5 1.4 fusion.7
  293.9 0.7 slice.30
  294.6 0.7 slice_bitcast_fusion
  295.3 0.6 copy.23
  295.9 0.6 reshape.130
  296.5 2.1 slice_convert_fusion.3
  298.6 0.0 copy-start
  298.6 4.2 %slice_convert_fusion = f32[1024,1024]{1,0:T(8,128)} fusion(bf16[1280,1024]{1,0:T(8,128)(2,1)} %get-tuple-element.20), kind=kLoop, calls=%fused_computation.1 | loop fusion | flops 1048576 | bytes 6291456 | tf_op jit(solution)/shard_map/convert_element_type | solution.py:1024
  302.8 0.0 copy-done
  302.8 1.9 slice_convert_fusion.2
  304.7 0.0 copy-start.2
  304.7 2.6 slice_convert_fusion.1
  307.3 0.0 copy-done.2
  307.3 0.0 copy-start.1
  307.3 1.3 copy.26
  308.6 1.0 copy-done.1
  309.7 1.3 copy.27
  (3 shorter events, 0.0 us)
Async XLA Ops:
  2.0 9.5 %copy-start.3 = (s32[1024]{0:T(1024)}, s32[1024]{0:T(1024)S(1)}, u32[]{:S(2)}) copy-start(s32[1024]{0:T(1024)S(1)} %convert_reduce_fusion) | copy-start | bytes 12292
  298.6 4.2 %copy-start = (bf16[1024,1792]{1,0:T(8,128)(2,1)S(1)}, bf16[1024,1792]{1,0:T(8,128)(2,1)}, u32[]{:S(2)}) copy-start(bf16[1024,1792]{1,0:T(8,128)(2,1)} %get-tuple-element.19) | copy-start | bytes 11010052
  304.7 2.6 copy-start.2
  307.3 2.3 copy-start.1
